TPU v7x, 32 devices: a whole 2x2x4 slice. The times are simulated.
32 devices in a mesh: grp: 2 (over x), row: 16 (over z, y, core).
Axes of the slice: x: 2, y: 2, z: 4, core: 2. Of those that a mesh axis runs over, the one named last changes fastest.
Arguments:
- coupling_features: bfloat16 [1024, 512, 128], P(('grp', 'row')), parts along dimension 0, may hold values from -6 to 6
- aligned_features: bfloat16 [256, 512, 256], P(('grp', 'row')), parts along dimension 0, may hold values from -6 to 6
- aligned_entry_flags: int32 [256, 512], P('grp'), parts along dimension 0, may hold values 0 or 1
- amino_real_flags: int32 [1024], P('grp'), parts along dimension 0, may hold values from 0 to 1, as said below
- coupling_offset_matrix: bfloat16 [128, 8], replicated, may hold values from -3.5 to 3.5
- lookup_matrices: bfloat16 [256, 1024], replicated, may hold values from -0.75 to 0.75
- aligned_final_matrix: bfloat16 [256, 256], replicated, may hold values from -0.375 to 0.375
- product_factor_matrices: bfloat16 [256, 64], replicated, may hold values from -0.375 to 0.375
- product_final_matrix: bfloat16 [1024, 128], replicated, may hold values from -1 to 1
- trio_factor_matrices: bfloat16 [128, 640], replicated, may hold values from -0.5 to 0.5
- trio_final_matrix: bfloat16 [128, 128], replicated, may hold values from -0.5 to 0.5
- feedforward_expand: bfloat16 [128, 512], replicated, may hold values from -0.5 to 0.5
- feedforward_shrink: bfloat16 [512, 128], replicated, may hold values from -0.25 to 0.25
Outputs:
- msa_out: bfloat16 [256, 512, 256], P(('grp', 'row')), parts along dimension 0
- coupling_refreshed: bfloat16 [1024, 512, 128], P(('grp', 'row')), parts along dimension 0
There are 2 independent parts, one for each index of `grp`. A program takes and returns all parts, laid end to end along the dimension named above; an argument that names none is the same for every part. Nothing has to cross between parts.
Inputs may be any that keep to these rules, and one draw needn't show every extreme that they name: `amino_real_flags`: 1 on a prefix of at least 256 residues and 0 on the rest, which is never empty.
All inputs are finite; a program needn't handle non-finite values.
Results may differ from a plain program's by a relative error of at most 0.008.
The roundings to bfloat16 on the way count: a program that leaves them out, or rounds other values in their place, can miss the bound.
Values may be sent and summed in bfloat16 or wider, within the bound.
No kernel may reach another device: no remote copies, remote signals or barrier semaphores. Data moves between devices by JAX's collectives and lax.ppermute only.
A program may use at most 192 MiB of HBM per device.

v0:
```python
import jax
import jax.numpy as jnp
from jax import lax
from jax.sharding import PartitionSpec as P

EPSILON = 1e-05


def standardize_features(values, dimension=-1):
    values = values.astype(jnp.float32)
    centered = values - jnp.mean(values, axis=dimension, keepdims=True)
    variance = jnp.mean(centered * centered, axis=dimension, keepdims=True)
    return centered * lax.rsqrt(variance + EPSILON)


def apply_matrix_map(values, weight):
    return jnp.einsum("...c,cd->...d", values, weight, preferred_element_type=jnp.float32)


def project_outer(raw_outer, product_final_matrix):
    row_total, col_total, left_width, right_width = raw_outer.shape
    flat = raw_outer.astype(jnp.bfloat16).reshape(row_total, col_total, left_width * right_width)
    return apply_matrix_map(flat, product_final_matrix)


def body(
    coupling_features,
    aligned_features,
    aligned_entry_flags,
    amino_real_flags,
    coupling_offset_matrix,
    lookup_matrices,
    aligned_final_matrix,
    product_factor_matrices,
    product_final_matrix,
    trio_factor_matrices,
    trio_final_matrix,
    feedforward_expand,
    feedforward_shrink,
):
    owned_aligned_lines = coupling_features.shape[0]
    residues = coupling_features.shape[1]
    pair_width = coupling_features.shape[2]
    owned_aligned_seqs = aligned_features.shape[0]
    aligned_feature_dim = aligned_features.shape[2]
    subspace_tally = coupling_offset_matrix.shape[1]
    subspace_dimension = aligned_feature_dim // subspace_tally
    outer_width = product_factor_matrices.shape[1] // 2
    placement_index = lax.axis_index("row")
    amino_real_valid = amino_real_flags.astype(jnp.float32)
    aligned_entry_valid = aligned_entry_flags.astype(jnp.float32) * amino_real_valid[None, :]
    my_residues = lax.dynamic_slice_in_dim(
        amino_real_valid, placement_index * owned_aligned_lines, owned_aligned_lines, 0
    )
    pair_valid = my_residues[:, None] * amino_real_valid[None, :]
    owned_aligned_flags = lax.dynamic_slice_in_dim(
        aligned_entry_valid, placement_index * owned_aligned_seqs, owned_aligned_seqs, 0
    )
    pair_normed = standardize_features(coupling_features).astype(jnp.bfloat16)
    bias_local = jnp.einsum(
        "ijc,ch->hij", pair_normed, coupling_offset_matrix, preferred_element_type=jnp.float32
    ).astype(jnp.bfloat16)
    tri_gates = jnp.einsum(
        "ijc,cd->dij",
        pair_normed,
        trio_factor_matrices[:, 0 : 4 * pair_width],
        preferred_element_type=jnp.float32,
    )
    left_tri = (
        jax.nn.sigmoid(tri_gates[0:pair_width])
        * tri_gates[pair_width : 2 * pair_width]
        * pair_valid[None]
    ).astype(jnp.bfloat16)
    right_tri = (
        jax.nn.sigmoid(tri_gates[2 * pair_width : 3 * pair_width])
        * tri_gates[3 * pair_width : 4 * pair_width]
        * pair_valid[None]
    ).astype(jnp.bfloat16)
    out_gate = jax.nn.sigmoid(
        apply_matrix_map(pair_normed, trio_factor_matrices[:, 4 * pair_width : 5 * pair_width])
    )
    left_full, right_full = (
        lax.all_to_all(left_tri, "row", split_axis=0, concat_axis=1, tiled=True),
        lax.all_to_all(right_tri, "row", split_axis=0, concat_axis=1, tiled=True),
    )
    tri_sum = jnp.einsum(
        "cik,cjk->cij", left_full, right_full, preferred_element_type=jnp.float32
    ).astype(jnp.bfloat16)
    tri_back = lax.all_to_all(tri_sum, "row", split_axis=1, concat_axis=0, tiled=True)
    tri_normed = standardize_features(tri_back, 0).astype(jnp.bfloat16)
    tri_update = out_gate * jnp.einsum(
        "cij,ce->ije", tri_normed, trio_final_matrix, preferred_element_type=jnp.float32
    )
    pair_one = coupling_features.astype(jnp.float32) + tri_update
    trans_hidden = jnp.maximum(
        apply_matrix_map(standardize_features(pair_one).astype(jnp.bfloat16), feedforward_expand),
        0.0,
    ).astype(jnp.bfloat16)
    pair_two = pair_one + apply_matrix_map(trans_hidden, feedforward_shrink)
    aligned_standardized = standardize_features(aligned_features).astype(jnp.bfloat16)
    lookup_factors_all = apply_matrix_map(aligned_standardized, lookup_matrices)
    asking_vectors = (
        (lookup_factors_all[..., 0:aligned_feature_dim] * subspace_dimension ** (-0.5))
        .astype(jnp.bfloat16)
        .reshape(owned_aligned_seqs, residues, subspace_tally, subspace_dimension)
    )
    lookup_subspaces = (
        lookup_factors_all[..., aligned_feature_dim : 2 * aligned_feature_dim]
        .astype(jnp.bfloat16)
        .reshape(owned_aligned_seqs, residues, subspace_tally, subspace_dimension)
    )
    content_subspaces = (
        lookup_factors_all[..., 2 * aligned_feature_dim : 3 * aligned_feature_dim]
        .astype(jnp.bfloat16)
        .reshape(owned_aligned_seqs, residues, subspace_tally, subspace_dimension)
    )
    aligned_sigmoid_factor = jax.nn.sigmoid(
        lookup_factors_all[..., 3 * aligned_feature_dim : 4 * aligned_feature_dim]
    )
    bias_piece = lax.all_gather(bias_local, "row", axis=1, tiled=True)
    asking_rows_sum = bias_piece.shape[1]
    affinity_matrix = jnp.einsum(
        "sihd,sjhd->shij", asking_vectors, lookup_subspaces, preferred_element_type=jnp.float32
    )
    affinity_matrix = affinity_matrix + bias_piece[None].astype(jnp.float32)
    affinity_matrix = jnp.where(
        owned_aligned_flags[:, None, None, :] > 0, affinity_matrix, -1000000000.0
    )
    attn_weights = jax.nn.softmax(affinity_matrix, axis=-1).astype(jnp.bfloat16)
    combined_features = jnp.einsum(
        "shij,sjhd->sihd", attn_weights, content_subspaces, preferred_element_type=jnp.float32
    )
    softmax_mixed_result = (
        combined_features.reshape(owned_aligned_seqs, asking_rows_sum, aligned_feature_dim)
        * aligned_sigmoid_factor
    ).astype(jnp.bfloat16)
    aligned_refreshed = aligned_features.astype(jnp.float32) + apply_matrix_map(
        softmax_mixed_result, aligned_final_matrix
    )
    product_standardized = standardize_features(aligned_refreshed).astype(jnp.bfloat16)
    product_factors = (
        jnp.einsum(
            "slm,mc->scl",
            product_standardized,
            product_factor_matrices,
            preferred_element_type=jnp.float32,
        )
        * owned_aligned_flags[:, None, :]
    )
    left_opm = product_factors[:, 0:outer_width].astype(jnp.bfloat16)
    right_opm = product_factors[:, outer_width : 2 * outer_width].astype(jnp.bfloat16)
    owned_crop_sites = lax.dynamic_slice_in_dim(
        aligned_entry_valid, placement_index * owned_aligned_lines, owned_aligned_lines, 1
    )
    coupling_tally = jnp.dot(
        owned_crop_sites.T, aligned_entry_valid, precision=lax.Precision.HIGHEST
    )
    left_res = lax.all_to_all(left_opm, "row", split_axis=2, concat_axis=0, tiled=True)
    right_all = lax.all_gather(right_opm, "row", axis=0, tiled=True)
    raw_total = jnp.einsum("sci,sdj->ijcd", left_res, right_all, preferred_element_type=jnp.float32)
    opm_sum = project_outer(raw_total, product_final_matrix)
    coupling_refreshed = (pair_two + opm_sum / jnp.maximum(coupling_tally, 1.0)[..., None]).astype(
        jnp.bfloat16
    )
    return (aligned_refreshed.astype(jnp.bfloat16), coupling_refreshed)


def solution(mesh):
    return jax.shard_map(
        body,
        mesh=mesh,
        in_specs=(
            P(("grp", "row"), None, None),
            P(("grp", "row"), None, None),
            P("grp", None),
            P("grp"),
            P(),
            P(),
            P(),
            P(),
            P(),
            P(),
            P(),
            P(),
            P(),
        ),
        out_specs=(P(("grp", "row"), None, None), P(("grp", "row"), None, None)),
        check_vma=False,
    )
```

profile of v0, /device:TPU:13, one launch (start us, length us, event | category | flops | bytes accessed | tf_op | source)
XLA Modules:
  0.0 526.4 jit_solution(14875835274564698252)
XLA Ops:
  7.2 6.5 %copy.75 = bf16[32,512,128]{1,2,0:T(8,128)(2,1)} copy(bf16[32,512,128]{2,1,0:T(8,128)(2,1)} %param.13) | data formatting | bytes 8388608 | tf_op args[0]
  20.6 15.8 %convolution_bitcast_fusion = f32[512,32,512]{0,2,1:T(8,128)} fusion(bf16[32,512,128]{1,2,0:T(8,128)(2,1)} %copy.75, f32[32,512]{1,0:T(8,128)S(1)} %add_rsqrt_fusion.2, f32[32,512]{1,0:T(8,128)S(1)} %broadcast_multiply_fusion.3, bf16[128,640]{1,0:T(8,128)(2,1)S(1)} %copy-done.12), kind=kOutput, calls=%fused_computation.13 | convolution fusion | flops 2155872256 | bytes 38010880 | tf_op jit(solution)/shard_map/ijc,cd->dij/dot_general | solution.py:63
  36.4 15.5 %fusion.15 = (bf16[128,32,512]{0,2,1:T(8,128)(2,1)}, bf16[128,32,512]{0,2,1:T(8,128)(2,1)}) fusion(f32[512,32,512]{0,2,1:T(8,128)} %convolution_bitcast_fusion, f32[32,512]{1,0:T(8,128)S(1)} %broadcast_multiply_fusion), kind=kLoop, calls=%fused_computation.24 | loop fusion | flops 25165824 | bytes 42008576 | tf_op jit(solution)/shard_map/convert_element_type | solution.py:78
  51.9 8.0 %copy.84 = bf16[128,32,512]{2,1,0:T(8,128)(2,1)} copy(bf16[128,32,512]{0,2,1:T(8,128)(2,1)} %get-tuple-element.11) | data formatting | bytes 8388608 | tf_op jit(solution)/shard_map/convert_element_type | solution.py:73
  59.9 7.2 %all-to-all-start = ((bf16[128,32,512]{2,1,0:T(8,128)(2,1)}), bf16[128,32,512]{2,1,0:T(8,128)(2,1)}, u32[]{:S(2)}, u32[]{:S(2)}) async-start(bf16[128,32,512]{2,1,0:T(8,128)(2,1)} %copy.84), calls=%async_computation | async-start | bytes 8388608 | tf_op jit(solution)/shard_map/all_to_all | solution.py:83
  70.9 8.2 %fusion.90 = (bf16[8,512,1024]{2,1,0:T(8,128)(2,1)S(1)}, f32[8,512,1024]{2,1,0:T(8,128)}) fusion(bf16[256,1024]{1,0:T(8,128)(2,1)S(1)} %copy-done, bf16[8,512,256]{1,2,0:T(8,128)(2,1)S(1)} %copy.70, f32[8,512]{1,0:T(8,128)S(1)} %add_rsqrt_fusion.4, f32[8,512]{1,0:T(8,128)S(1)} %broadcast_multiply_fusion.5), kind=kOutput, calls=%fused_computation.117 | convolution fusion | flops 2155872256 | bytes 27820032 | tf_op jit(solution)/shard_map/...c,cd->...d/dot_general | solution.py:17
  81.6 3.9 copy.72
  85.5 4.0 fusion.39
  89.5 3.9 copy.73
  93.5 3.9 copy.74
  97.4 7.9 %copy.86 = bf16[128,32,512]{2,1,0:T(8,128)(2,1)} copy(bf16[128,32,512]{0,2,1:T(8,128)(2,1)} %get-tuple-element.10) | data formatting | bytes 8388608 | tf_op jit(solution)/shard_map/convert_element_type | solution.py:78
  105.4 8.7 %copy.77 = f32[8,512,512]{1,2,0:T(8,128)} copy(bf16[8,512,512]{2,0,1:T(8,128)(2,1)} %all-gather.3.cloned.1.call-done) | data formatting | bytes 12582912 | tf_op jit(solution)/shard_map/convert_element_type | solution.py:125
  114.2 39.5 %fusion.91 = (f32[8,8,512]{2,1,0:T(8,128)S(1)}, f32[8,8,512,512]{2,3,1,0:T(8,128)}) fusion(f32[8,512,512]{1,2,0:T(8,128)} %copy.77, pred[8,512]{1,0:T(8,128)(4,1)S(1)} %get-tuple-element.8, bf16[8,512,8,32]{1,3,2,0:T(8,128)(2,1)} %bitcast.101, bf16[8,512,8,32]{1,3,2,0:T(8,128)(2,1)} %bitcast.102), kind=kOutput, calls=%fused_computation.118 | convolution fusion | flops 1140851200 | bytes 79826944 | tf_op jit(solution)/shard_map/sub | solution.py:129
  153.6 6.1 %all-to-all-done = bf16[128,32,512]{2,1,0:T(8,128)(2,1)} async-done(((bf16[128,32,512]{2,1,0:T(8,128)(2,1)}), bf16[128,32,512]{2,1,0:T(8,128)(2,1)}, u32[]{:S(2)}, u32[]{:S(2)}) %all-to-all-start) | async-done | bytes 4194336 | tf_op jit(solution)/shard_map/all_to_all | solution.py:83
  159.8 5.5 %all-to-all-start.1 = ((bf16[128,32,512]{2,1,0:T(8,128)(2,1)}), bf16[128,32,512]{2,1,0:T(8,128)(2,1)}, u32[]{:S(2)}, u32[]{:S(2)}) async-start(bf16[128,32,512]{2,1,0:T(8,128)(2,1)} %copy.86), calls=%async_computation.1 | async-start | bytes 8388608 | tf_op jit(solution)/shard_map/all_to_all | solution.py:84
  165.3 24.5 %fusion.5 = f32[8,8,32,512]{3,2,1,0:T(8,128)} fusion(bf16[8,512,8,32]{1,3,2,0:T(8,128)(2,1)} %bitcast.110, f32[8,8,512,512]{2,3,1,0:T(8,128)} %get-tuple-element.21, f32[8,8,512]{2,1,0:T(8,128)S(1)} %get-tuple-element.20), kind=kOutput, calls=%fused_computation.10 | convolution fusion | flops 1107296256 | bytes 73531392 | tf_op jit(solution)/shard_map/shij,sjhd->sihd/dot_general | solution.py:130
  189.8 5.3 %copy.79 = f32[8,512,256]{2,1,0:T(8,128)} copy(f32[8,512,256]{1,2,0:T(8,128)} %bitcast.109) | data formatting | bytes 8388608 | tf_op jit(solution)/shard_map/reshape | solution.py:134
  195.1 4.9 copy.85
  200.0 5.8 %fusion.92 = (f32[8,512]{1,0:T(8,128)S(1)}, f32[8,512,256]{1,2,0:T(8,128)}) fusion(bf16[256,256]{1,0:T(8,128)(2,1)S(1)} %copy-done.17, f32[8,512,256]{2,1,0:T(8,128)S(1)} %copy-done.6, f32[8,512,1024]{2,1,0:T(8,128)} %get-tuple-element.19, bf16[8,512,256]{1,2,0:T(8,128)(2,1)S(1)} %copy.70), kind=kOutput, calls=%fused_computation.119 | convolution fusion | flops 545255424 | bytes 14827520 | tf_op jit(solution)/shard_map/...c,cd->...d/dot_general | solution.py:17
  205.8 51.8 %all-to-all-done.1 = bf16[128,32,512]{2,1,0:T(8,128)(2,1)} async-done(((bf16[128,32,512]{2,1,0:T(8,128)(2,1)}), bf16[128,32,512]{2,1,0:T(8,128)(2,1)}, u32[]{:S(2)}, u32[]{:S(2)}) %all-to-all-start.1) | async-done | bytes 4194336 | tf_op jit(solution)/shard_map/all_to_all | solution.py:84
  257.6 4.9 copy.87
  269.3 4.8 all-to-all-start.3
  274.1 5.8 %convolution_convert_fusion = bf16[8,512,512]{2,1,0:T(8,128)(2,1)S(1)} fusion(bf16[8,512,512]{2,1,0:T(8,128)(2,1)} %bitcast.107, bf16[8,512,512]{2,1,0:T(8,128)(2,1)} %bitcast.108), kind=kOutput, calls=%fused_computation.69 | convolution fusion | flops 2149580800 | bytes 12582912 | tf_op jit(solution)/shard_map/cik,cjk->cij/dot_general | solution.py:86
  279.9 4.4 copy.88
  284.3 6.0 %all-to-all-start.2 = ((bf16[8,512,512]{2,0,1:T(8,128)(2,1)}), bf16[8,512,512]{2,0,1:T(8,128)(2,1)}, u32[]{:S(2)}, u32[]{:S(2)}) async-start(bf16[8,512,512]{2,0,1:T(8,128)(2,1)} %copy.88), calls=%async_computation.2 | async-start | bytes 8388608 | tf_op jit(solution)/shard_map/all_to_all | solution.py:89
  296.2 111.9 %all-to-all-done.2 = bf16[8,512,512]{2,0,1:T(8,128)(2,1)} async-done(((bf16[8,512,512]{2,0,1:T(8,128)(2,1)}), bf16[8,512,512]{2,0,1:T(8,128)(2,1)}, u32[]{:S(2)}, u32[]{:S(2)}) %all-to-all-start.2) | async-done | bytes 4194336 | tf_op jit(solution)/shard_map/all_to_all | solution.py:89
  418.4 4.7 fusion.93
  426.3 20.6 %convert_bitcast_fusion = bf16[32,512,32,32]{1,0,2,3:T(8,128)(2,1)} fusion(bf16[128,32,512,1]{2,1,0,3:T(8,128)(2,1)} %bitcast.103, bf16[128,32,32]{0,2,1:T(8,128)(2,1)S(1)} %copy.97), kind=kOutput, calls=%fused_computation.5 | convolution fusion | flops 4311744512 | bytes 38010880 | tf_op jit(solution)/shard_map/sci,sdj->ijcd/dot_general | solution.py:160
  446.9 31.4 %copy.98 = bf16[32,512,32,32]{1,3,2,0:T(8,128)(2,1)} copy(bf16[32,512,32,32]{1,0,2,3:T(8,128)(2,1)} %convert_bitcast_fusion) | data formatting | bytes 67108864 | tf_op jit(solution)/shard_map/convert_element_type | solution.py:22
  478.3 14.3 %fusion.6 = f32[32,512,128]{1,2,0:T(8,128)} fusion(f32[32,512,128]{1,2,0:T(8,128)} %copy-done.5, f32[32,512]{1,0:T(8,128)S(1)} %add_rsqrt_fusion, f32[32,512]{1,0:T(8,128)S(1)} %broadcast_multiply_fusion.1, bf16[512,128]{1,0:T(8,128)(2,1)S(1)} %copy-done.18, bf16[128,512]{1,0:T(8,128)(2,1)S(1)} %copy-done.19), kind=kOutput, calls=%fused_computation.11 | convolution fusion | flops 4318035968 | bytes 17170432 | tf_op jit(solution)/shard_map/...c,cd->...d/dot_general | solution.py:17
  492.7 20.1 %add_convert_fusion = bf16[32,512,128]{1,2,0:T(8,128)(2,1)} fusion(f32[32,512,128]{1,2,0:T(8,128)} %copy-done.5, f32[32,512,128]{1,2,0:T(8,128)} %fusion.6, f32[32,512]{1,0:T(8,128)S(1)} %convolution_maximum_fusion, bf16[32,512,1024]{1,2,0:T(8,128)(2,1)} %bitcast.100, bf16[1024,128]{1,0:T(8,128)(2,1)S(1)} %copy-done.16), kind=kOutput, calls=%fused_computation.40 | convolution fusion | flops 4303355904 | bytes 54853632 | tf_op jit(solution)/shard_map/...c,cd->...d/dot_general | solution.py:17
  512.7 6.4 %copy.102 = bf16[32,512,128]{2,1,0:T(8,128)(2,1)} copy(bf16[32,512,128]{1,2,0:T(8,128)(2,1)} %add_convert_fusion) | data formatting | bytes 8388608
  (85 shorter events, 39.3 us)
Async XLA Ops:
  7.2 63.8 %copy-start = (bf16[256,1024]{1,0:T(8,128)(2,1)S(1)}, bf16[256,1024]{1,0:T(8,128)(2,1)}, u32[]{:S(2)}) copy-start(bf16[256,1024]{1,0:T(8,128)(2,1)} %param.18) | copy-start | bytes 1572868
  7.2 98.2 %all-gather.3.cloned.1.call-start = ((), (), s32[]{:S(2)}) async-start(), calls=%async_computation.4 | async-start | bytes 4456448 | tf_op jit(solution)/shard_map/all_gather | solution.py:120
  13.7 3.4 copy-start.2
  13.7 4.8 copy-start.20
  17.1 3.4 copy-start.7
  18.5 1.9 copy-start.15
  18.5 2.1 copy-start.12
  18.6 17.8 %copy-start.9 = (f32[32,512]{1,0:T(8,128)}, f32[32,512]{1,0:T(8,128)S(1)}, u32[]{:S(2)}) copy-start(f32[32,512]{1,0:T(8,128)S(1)} %add_rsqrt_fusion.2) | copy-start | bytes 196612
  59.9 99.9 %all-to-all-start = ((bf16[128,32,512]{2,1,0:T(8,128)(2,1)}), bf16[128,32,512]{2,1,0:T(8,128)(2,1)}, u32[]{:S(2)}, u32[]{:S(2)}) async-start(bf16[128,32,512]{2,1,0:T(8,128)(2,1)} %copy.84), calls=%async_computation | async-start | bytes 8388608 | tf_op jit(solution)/shard_map/all_to_all | solution.py:83
  97.4 7.9 %copy-start.11 = (s32[128,512]{1,0:T(8,128)S(1)}, s32[128,512]{1,0:T(8,128)}, u32[]{:S(2)}) copy-start(s32[128,512]{1,0:T(8,128)} %param.15) | copy-start | bytes 786436
  159.8 97.8 %all-to-all-start.1 = ((bf16[128,32,512]{2,1,0:T(8,128)(2,1)}), bf16[128,32,512]{2,1,0:T(8,128)(2,1)}, u32[]{:S(2)}, u32[]{:S(2)}) async-start(bf16[128,32,512]{2,1,0:T(8,128)(2,1)} %copy.86), calls=%async_computation.1 | async-start | bytes 8388608 | tf_op jit(solution)/shard_map/all_to_all | solution.py:84
  195.1 4.9 copy-start.6
  195.1 4.9 copy-start.17
  257.6 4.9 copy-start.4
  262.5 0.8 copy-start.13
  269.3 15.0 %all-to-all-start.3 = ((bf16[16,2,4096]{2,1,0:T(2,128)(2,1)}), bf16[16,2,4096]{2,1,0:T(2,128)(2,1)S(1)}, u32[]{:S(2)}, u32[]{:S(2)}) async-start(bf16[16,2,4096]{2,1,0:T(2,128)(2,1)} %reshape.139), calls=%async_computation.3 | async-start | bytes 524288 | tf_op jit(solution)/shard_map/all_to_all | solution.py:158
  284.3 123.8 %all-to-all-start.2 = ((bf16[8,512,512]{2,0,1:T(8,128)(2,1)}), bf16[8,512,512]{2,0,1:T(8,128)(2,1)}, u32[]{:S(2)}, u32[]{:S(2)}) async-start(bf16[8,512,512]{2,0,1:T(8,128)(2,1)} %copy.88), calls=%async_computation.2 | async-start | bytes 8388608 | tf_op jit(solution)/shard_map/all_to_all | solution.py:89
  290.3 136.0 %all-gather.5.cloned.1.call-start = ((), (), s32[]{:S(2)}) async-start(), calls=%async_computation.5 | async-start | bytes 4456448 | tf_op jit(solution)/shard_map/all_gather | solution.py:159
  408.1 6.3 %copy-start.14 = (bf16[128,128]{1,0:T(8,128)(2,1)S(1)}, bf16[128,128]{1,0:T(8,128)(2,1)}, u32[]{:S(2)}) copy-start(bf16[128,128]{1,0:T(8,128)(2,1)} %param.23) | copy-start | bytes 98308
  414.4 3.9 copy-start.3
  414.4 3.9 copy-start.8
  414.4 3.9 copy-start.10
  423.1 3.2 copy-start.5
  446.9 31.4 %copy-start.18 = (bf16[512,128]{1,0:T(8,128)(2,1)S(1)}, bf16[512,128]{1,0:T(8,128)(2,1)}, u32[]{:S(2)}) copy-start(bf16[512,128]{1,0:T(8,128)(2,1)} %param.25) | copy-start | bytes 393220
  446.9 31.4 %copy-start.19 = (bf16[128,512]{1,0:T(8,128)(2,1)S(1)}, bf16[128,512]{1,0:T(8,128)(2,1)}, u32[]{:S(2)}) copy-start(bf16[128,512]{1,0:T(8,128)(2,1)} %param.24) | copy-start | bytes 393220
  478.3 14.3 %copy-start.16 = (bf16[1024,128]{1,0:T(8,128)(2,1)S(1)}, bf16[1024,128]{1,0:T(8,128)(2,1)}, u32[]{:S(2)}) copy-start(bf16[1024,128]{1,0:T(8,128)(2,1)} %param.21) | copy-start | bytes 786436
  492.7 26.5 %copy-start.1 = (bf16[256,1024]{1,0:T(8,128)(2,1)S(1)}, bf16[256,1024]{1,0:T(8,128)(2,1)}, u32[]{:S(2)}) copy-start(bf16[256,1024]{1,0:T(8,128)(2,1)} %param.18) | copy-start | bytes 1572868
Sparse Core Ops, SparseCore 0:
  20.5 51.0 all-gather.2
  293.3 94.7 all-gather.4
where the time goes:
time: 534 us; the launch traced here: 526 us
  waiting for transfers between devices  170 us (32%)
  matrix products  166 us (31%)
  local copies, waits for them, and re-layouts  118 us (22%)
  other arithmetic  33.3 us (6%)
  starting transfers between devices  23.8 us (4%)
  between operations  14.9 us (3%)
    all_to_all x1, waiting for transfers between devices, body(): lax.all_to_all(tri_sum, 'row', split_axis=1, concat_axis=0, tiled=True)  112 us
    dot_general x5, matrix products, apply_matrix_map(): jnp.einsum('...c,cd->...d', values, weight, preferred_element_type=jnp.fl...  53.1 us
    all_to_all x1, waiting for transfers between devices, body(): lax.all_to_all(right_tri, 'row', split_axis=0, concat_axis=1, tiled=True)  51.8 us
    sub x1, matrix products, body(): attn_weights = jax.nn.softmax(affinity_matrix, axis=-1).astype(jnp.bfloat16)  39.5 us
    convert_element_type x1, local copies, waits for them, and re-layouts, project_outer(): raw_outer.astype(jnp.bfloat16)  31.4 us
    dot_general x1, matrix products, body(): jnp.einsum('shij,sjhd->sihd', attn_weights, content_subspaces, preferred_...  24.5 us
    unnamed x48, local copies, waits for them, and re-layouts  24 us
    dot_general x1, matrix products, body(): jnp.einsum('sci,sdj->ijcd', left_res, right_all, preferred_element_type=j...  20.6 us
  transfers between devices with their start and end apart: 6, of which 3 were waited for; matrix products, arithmetic and copies ran while one was open for 38% of the time, Pallas kernels for 0%

commit v1 on v0

v1 whole, which is shorter than its diff:
```python
import functools

import jax
import jax.numpy as jnp
from jax import lax
from jax.experimental import pallas as pl
from jax.experimental.pallas import tpu as pltpu
from jax.sharding import PartitionSpec as P


EPSILON = 1e-05
F32 = jnp.float32
BF16 = jnp.bfloat16
LANES = 128
HEAD_UNROLL = 4
TAIL_UNROLL = 4


def norm(values, axis=-1):
    centered = values - jnp.mean(values, axis=axis, keepdims=True)
    variance = jnp.mean(centered * centered, axis=axis, keepdims=True)
    return centered * lax.rsqrt(variance + EPSILON)


def dot(a, b, ca=1, cb=0):
    return lax.dot_general(a, b, (((ca,), (cb,)), ((), ())), preferred_element_type=F32)


def divisor(total, limit):
    best = min(total, limit)
    while total % best:
        best -= 1
    return best


def put_rows(scr, first, rows, values):
    for n in range(scr.shape[0]):
        scr[n, pl.ds(first, values.shape[0], stride=rows), :] = values[:, n * LANES : (n + 1) * LANES]


def get_rows(scr, first, rows):
    count = scr.shape[1] // rows
    return jnp.concatenate([scr[n, pl.ds(first, count, stride=rows), :] for n in range(scr.shape[0])], axis=1)


def full(shape):
    return pl.BlockSpec(shape, lambda *_: (0,) * len(shape))


def head_kernel(rows, with_bias, x_ref, vi_ref, vj_ref, w_ref, *refs):
    if with_bias:
        wb_ref, tri_ref, bias_ref, scr = refs
    else:
        tri_ref, scr = refs
    cz = x_ref.shape[2]
    heads = wb_ref.shape[0] if with_bias else 0

    def row(i, carry):
        xn = norm(x_ref[i].astype(F32)).astype(BF16)
        both = dot(w_ref[...], xn, 1, 1)
        valid = vj_ref[...] * vi_ref[0, i]
        put_rows(scr, i, rows, jax.nn.sigmoid(both[0:cz]) * both[cz : 2 * cz] * valid)
        if with_bias:
            put_rows(scr, cz * rows + i, rows, dot(wb_ref[...], xn, 1, 1))
        return carry

    lax.fori_loop(0, rows, row, 0, unroll=HEAD_UNROLL)
    for n in range(scr.shape[0]):
        cols = slice(n * LANES, (n + 1) * LANES)
        tri_ref[:, :, cols] = scr[n, 0 : cz * rows].astype(BF16).reshape(cz, rows, LANES)
        if with_bias:
            bias_ref[:, :, cols] = scr[n, cz * rows :].astype(BF16).reshape(heads, rows, LANES)


def pair_head(x, my_valid, valid, w, wb=None, part=0, parts=1):
    owned, res, cz = x.shape
    owned = owned // parts
    rows = divisor(owned, 16)
    steps = owned // rows
    heads = 0 if wb is None else wb.shape[0]
    in_specs = [
        pl.BlockSpec((rows, res, cz), lambda g: (g + part * steps, 0, 0)),
        pl.BlockSpec((1, 1, rows), lambda g: (g + part * steps, 0, 0), memory_space=pltpu.SMEM),
        full((1, res)),
        full(w.shape),
    ]
    args = [x, my_valid.reshape(-1, 1, rows), valid.reshape(1, res), w]
    out_specs = [pl.BlockSpec((cz, rows, res), lambda g: (0, g, 0))]
    out_shape = [jax.ShapeDtypeStruct((cz, owned, res), BF16)]
    if heads:
        in_specs.append(full(wb.shape))
        args.append(wb)
        out_specs.append(pl.BlockSpec((heads, rows, res), lambda g: (0, g, 0)))
        out_shape.append(jax.ShapeDtypeStruct((heads, owned, res), BF16))

    def kernel(x_ref, vi_ref, vj_ref, w_ref, *refs):
        head_kernel(rows, heads > 0, x_ref, vi_ref.at[0], vj_ref, w_ref, *refs)

    return pl.pallas_call(
        kernel,
        grid=(steps,),
        in_specs=in_specs,
        out_specs=out_specs,
        out_shape=out_shape,
        scratch_shapes=[pltpu.VMEM((res // LANES, (cz + heads) * rows, LANES), F32)],
        name="pair_head_bias" if heads else "pair_head",
    )(*args)


def msa_kernel(width, chunk, x_ref, valid_ref, bias_ref, w_ref, wf_ref, wp_ref, o_ref, l_ref, r_ref, q_s, k_s, v_s, att):
    res, feat = x_ref.shape[1:]
    half = feat // 2
    per_half = half // width
    x = x_ref[0].astype(F32)
    xn = norm(x).astype(BF16)
    q_s[...] = (dot(xn, w_ref[:, 0:feat]) * width ** (-0.5)).astype(BF16)
    k_s[...] = dot(xn, w_ref[:, feat : 2 * feat]).astype(BF16)
    v_s[...] = dot(xn, w_ref[:, 2 * feat : 3 * feat]).astype(BF16)
    valid = valid_ref[0]
    lane = lax.broadcasted_iota(jnp.int32, (1, feat), 1) // width
    lane_half = lax.broadcasted_iota(jnp.int32, (1, half), 1) // width

    def heads(step, carry):
        for side in (0, 1):
            mine = lane == step + side * per_half
            mine_half = lane_half == step
            v = jnp.where(mine, v_s[...], jnp.ones((), BF16))
            for c in range(res // chunk):
                span = slice(c * chunk, (c + 1) * chunk)
                q = jnp.where(mine, q_s[span], jnp.zeros((), BF16))
                s = dot(q, k_s[...], 1, 1) + bias_ref[step + side * per_half, span].astype(F32)
                s = jnp.where(valid > 0, s, -1000000000.0)
                p = jnp.exp(s - jnp.max(s, axis=1, keepdims=True)).astype(BF16)
                out = dot(p, v)
                mixed = out[:, side * half : (side + 1) * half] / out[:, (1 - side) * half : (2 - side) * half]
                cols = slice(side * half, (side + 1) * half)
                att[span, cols] = jnp.where(mine_half, mixed, att[span, cols])
        return carry

    lax.fori_loop(0, per_half, heads, 0)
    gate = jax.nn.sigmoid(dot(xn, w_ref[:, 3 * feat : 4 * feat]))
    mixed = (att[...] * gate).astype(BF16)
    new = x + dot(mixed, wf_ref[...])
    o_ref[0] = new.astype(BF16)
    factors = dot(wp_ref[...], norm(new).astype(BF16), 1, 1) * valid
    outer = l_ref.shape[1]
    l_ref[0] = factors[0:outer].astype(BF16)
    r_ref[0] = factors[outer : 2 * outer].astype(BF16)


def msa_block(x, valid, bias, w, wf, wp, width):
    seqs, res, feat = x.shape
    outer = wp.shape[0] // 2
    return pl.pallas_call(
        functools.partial(msa_kernel, width, divisor(res, 256)),
        grid=(seqs,),
        in_specs=[
            pl.BlockSpec((1, res, feat), lambda s: (s, 0, 0)),
            pl.BlockSpec((1, 1, res), lambda s: (s, 0, 0)),
            full(bias.shape),
            full(w.shape),
            full(wf.shape),
            full(wp.shape),
        ],
        out_specs=[
            pl.BlockSpec((1, res, feat), lambda s: (s, 0, 0)),
            pl.BlockSpec((1, outer, res), lambda s: (s, 0, 0)),
            pl.BlockSpec((1, outer, res), lambda s: (s, 0, 0)),
        ],
        out_shape=[
            jax.ShapeDtypeStruct((seqs, res, feat), BF16),
            jax.ShapeDtypeStruct((seqs, outer, res), BF16),
            jax.ShapeDtypeStruct((seqs, outer, res), BF16),
        ],
        scratch_shapes=[pltpu.VMEM((res, feat), BF16)] * 3 + [pltpu.VMEM((res, feat), F32)],
        name="msa_block",
    )(x, valid.reshape(seqs, 1, res), bias, w, wf, wp)


def tri_kernel(l_ref, *refs):
    groups, chans, owned, res = l_ref.shape
    o_ref = refs[-1]
    for c in range(chans):
        a = l_ref[:, c].reshape(groups * owned, res)
        for n, r_ref in enumerate(refs[:-1]):
            count = groups * r_ref.shape[2]
            part = dot(a, r_ref[:, c].reshape(count, res), 1, 1).astype(BF16)
            o_ref[:, c, :, n * count : (n + 1) * count] = part.reshape(groups, owned, count)


def tri_sums(left, rights):
    groups, chans, owned, res = left.shape
    step = divisor(chans, 4)

    def spec(rows, cols):
        return pl.BlockSpec((groups, step, rows, cols), lambda c: (0, c, 0, 0))

    cols = groups * sum(r.shape[2] for r in rights)
    return pl.pallas_call(
        tri_kernel,
        grid=(chans // step,),
        in_specs=[spec(owned, res)] + [spec(r.shape[2], res) for r in rights],
        out_specs=spec(owned, cols),
        out_shape=jax.ShapeDtypeStruct((groups, chans, owned, cols), BF16),
        name="tri_sums",
    )(left, *rights)


def opm_kernel(l_ref, r_ref, w_ref, vt_ref, vi_ref, o_ref, mix):
    rows, seqs, outer = l_ref.shape
    cz = o_ref.shape[2]
    inner = w_ref.shape[1] // cz
    for first in range(0, rows, 2):
        pair = min(2, rows - first)
        both = l_ref[first : first + pair].reshape(pair * seqs, outer)
        for d in range(inner):
            part = dot(both, w_ref[:, d * cz : (d + 1) * cz]).astype(BF16)
            for n in range(pair):
                mix[d * seqs : (d + 1) * seqs, n * cz : (n + 1) * cz] = part[n * seqs : (n + 1) * seqs]
        total = dot(r_ref[...], mix[:, 0 : pair * cz])
        for n in range(pair):
            mine = jnp.broadcast_to(vi_ref[:, first + n : first + n + 1], (seqs, cz)).astype(BF16)
            tally = jnp.maximum(dot(vt_ref[...], mine), 1.0)
            o_ref[first + n] = total[:, n * cz : (n + 1) * cz] / tally


def opm_block(left, right, w, valid_t, mine):
    owned, seqs, outer = left.shape
    res, depth = right.shape
    cz = w.shape[1] // (depth // seqs)
    rows = divisor(owned, 8)
    return pl.pallas_call(
        opm_kernel,
        grid=(owned // rows,),
        in_specs=[
            pl.BlockSpec((rows, seqs, outer), lambda g: (g, 0, 0)),
            full(right.shape),
            full(w.shape),
            full(valid_t.shape),
            pl.BlockSpec((None, seqs, rows), lambda g: (g, 0, 0)),
        ],
        out_specs=pl.BlockSpec((rows, res, cz), lambda g: (g, 0, 0)),
        out_shape=jax.ShapeDtypeStruct((owned, res, cz), F32),
        scratch_shapes=[pltpu.VMEM((depth, 2 * cz), BF16)],
        name="opm_block",
    )(left, right, w, valid_t, mine.reshape(seqs, owned // rows, rows).transpose(1, 0, 2))


def tail_kernel(half_ref, x_ref, tri_ref, opm_ref, wg_ref, wt_ref, w1_ref, w2_ref, *refs):
    o_ref, scr = refs[-2:]
    rows, groups, lines, cz = x_ref.shape
    for n in range(scr.shape[0]):
        part = tri_ref[:, :, n * LANES : (n + 1) * LANES]
        scr[n] = part.astype(F32).reshape(scr.shape[1:])

    def row(i, carry):
        x = x_ref[i].reshape(groups * lines, cz).astype(F32)
        gate = jax.nn.sigmoid(dot(norm(x).astype(BF16), wg_ref[...]))
        tri = norm(get_rows(scr, i, rows), 0).astype(BF16)
        one = x + gate * dot(tri, wt_ref[...], 0, 0)
        hidden = jnp.maximum(dot(norm(one).astype(BF16), w1_ref[...]), 0.0).astype(BF16)
        out = one + dot(hidden, w2_ref[...]) + opm_ref[i].reshape(groups * lines, cz)
        o_ref[i] = out.astype(BF16).reshape(groups, lines, cz)
        return carry

    lax.fori_loop(0, rows, row, 0, unroll=TAIL_UNROLL)


def pair_tail(half, first, parts, x, tri, opm, wg, wt, w1, w2, earlier=None):
    owned, res, cz = x.shape
    ring = res // owned
    rows = divisor(owned, 16)
    lines = owned // parts
    span = ring // 2 * lines
    count = tri.shape[2] // span
    view = (owned, ring, parts, lines, cz)
    pair = pl.BlockSpec((rows, ring // 2, None, lines, cz), lambda q, g, h: (g, h[0], first + q, 0, 0))
    in_specs = [
        pair,
        pl.BlockSpec((cz, rows, span), lambda q, g, h: (0, g, q)),
        pair,
        full(wg.shape),
        full(wt.shape),
        full(w1.shape),
        full(w2.shape),
    ]
    args = [half, x.reshape(view), tri, opm.reshape(view), wg, wt, w1, w2]
    if earlier is not None:
        in_specs.append(pl.BlockSpec(memory_space=pl.ANY))
        args.append(earlier.reshape(view))
    return pl.pallas_call(
        tail_kernel,
        grid_spec=pltpu.PrefetchScalarGridSpec(
            num_scalar_prefetch=1,
            grid=(count, owned // rows),
            in_specs=in_specs,
            out_specs=pair,
            scratch_shapes=[pltpu.VMEM((max(span // LANES, 1), cz * rows, min(span, LANES)), F32)],
        ),
        out_shape=jax.ShapeDtypeStruct(view, BF16),
        input_output_aliases={} if earlier is None else {8: 0},
        name="pair_tail",
    )(*args).reshape(owned, res, cz)


def body(
    ring,
    coupling_features,
    aligned_features,
    aligned_entry_flags,
    amino_real_flags,
    coupling_offset_matrix,
    lookup_matrices,
    aligned_final_matrix,
    product_factor_matrices,
    product_final_matrix,
    trio_factor_matrices,
    trio_final_matrix,
    feedforward_expand,
    feedforward_shrink,
):
    owned, res, cz = coupling_features.shape
    seqs, _, feat = aligned_features.shape
    width = feat // coupling_offset_matrix.shape[1]
    outer = product_factor_matrices.shape[1] // 2
    place = lax.axis_index("row")
    near = ring // 2
    halves = [list(range(near)), list(range(near, ring))]
    swap = [(r, (r + near) % ring) for r in range(ring)]

    residue = amino_real_flags.astype(F32)
    entry = aligned_entry_flags.astype(F32) * residue[None, :]
    my_residue = lax.dynamic_slice_in_dim(residue, place * owned, owned, 0)
    my_entry = lax.dynamic_slice_in_dim(entry, place * seqs, seqs, 0)
    trio = trio_factor_matrices.T

    parts = 2 if owned % 32 == 0 else 1
    half = (place // near).astype(jnp.int32).reshape(1)

    def spread(values):
        values = values.reshape(near, cz // near, values.shape[1], values.shape[-1])
        return lax.all_to_all(values, "row", 0, 0, tiled=True, axis_index_groups=halves)

    made = [
        pair_head(coupling_features, my_residue, residue, trio[2 * cz : 4 * cz], coupling_offset_matrix.T, part, parts)
        for part in range(parts)
    ]
    bias = jnp.concatenate([b for _, b in made], axis=1)
    right_own, right_oth = [], []
    for part in range(parts):
        right_own.append(spread(made[part][0]))
        right_oth.append(lax.ppermute(right_own[part], "row", swap))
    (left,) = pair_head(coupling_features, my_residue, residue, trio[0 : 2 * cz])
    left_own = spread(left)
    bias_all = lax.all_gather(bias, "row", axis=1, tiled=True)

    msa_out, left_opm, right_opm = msa_block(
        aligned_features,
        my_entry,
        bias_all,
        lookup_matrices,
        aligned_final_matrix,
        product_factor_matrices.T,
        width,
    )

    def collect(sums):
        back = lax.all_to_all(sums, "row", 0, 0, tiled=True, axis_index_groups=halves)
        return back.reshape(cz, owned, sums.shape[-1])

    sums = tri_sums(left_own, right_own)
    tri_own = collect(sums)
    tri_oth = []
    for part in range(parts):
        sums = tri_sums(left_own, [right_oth[part]])
        tri_oth.append(collect(sums))

    left_res = lax.all_to_all(left_opm, "row", split_axis=2, concat_axis=0, tiled=True).transpose(2, 0, 1)
    right_all = lax.all_gather(right_opm.transpose(1, 0, 2), "row", axis=1, tiled=True)
    right_all = right_all.reshape(outer * ring * seqs, res).T
    mine = lax.dynamic_slice_in_dim(entry, place * owned, owned, 1)
    opm = opm_block(left_res, right_all, product_final_matrix.reshape(outer, outer * cz), entry.T.astype(BF16), mine)
    weights = (trio_factor_matrices[:, 4 * cz : 5 * cz], trio_final_matrix, feedforward_expand, feedforward_shrink)
    pair = pair_tail(half, 0, parts, coupling_features, tri_own, opm, *weights)
    for part in range(parts):
        pair = pair_tail(1 - half, part, parts, coupling_features, tri_oth[part], opm, *weights, earlier=pair)
    return (msa_out, pair)


def solution(mesh):
    return jax.shard_map(
        functools.partial(body, mesh.shape["row"]),
        mesh=mesh,
        in_specs=(
            P(("grp", "row"), None, None),
            P(("grp", "row"), None, None),
            P("grp", None),
            P("grp"),
            P(),
            P(),
            P(),
            P(),
            P(),
            P(),
            P(),
            P(),
            P(),
        ),
        out_specs=(P(("grp", "row"), None, None), P(("grp", "row"), None, None)),
        check_vma=False,
    )
```

time: 534 us -> 519 us (0.972)
  Pallas kernels: 0 us -> 208 us
  matrix products: 166 us -> 0 us
  local copies, waits for them, and re-layouts: 118 us -> 32.1 us
  waiting for transfers between devices: 170 us -> 215 us
  other arithmetic: 33.3 us -> 2.2 us
  starting transfers between devices: 23.8 us -> 45 us
    pallas_call x0 -> x11, Pallas kernels: none -> 208 us  [the longest x3 77.5 us: pair_tail(): pl.pallas_call(tail_kernel, grid_spec=pltpu.PrefetchScalarGridSpec(num_sc...]
    dot_general x13 -> x0, matrix products: 126 us -> none  [the longest x5 53.1 us: apply_matrix_map(): jnp.einsum('...c,cd->...d', values, weight, preferred_element_type=jnp.fl...]
    all_to_all x3 -> x6, waiting for transfers between devices: 170 us -> 45.4 us  [the longest x3 31.9 us: spread(): lax.all_to_all(values, 'row', 0, 0, tiled=True, axis_index_groups=halves)]
    ppermute x0 -> x2, waiting for transfers between devices: none -> 91.4 us  [body(): right_oth.append(lax.ppermute(right_own[part], 'row', swap))]
    all_gather x2, waiting for transfers between devices: 0.04 us -> 70 us  [the longest x1 70 us: body(): bias_all = lax.all_gather(bias, 'row', axis=1, tiled=True)]
    convert_element_type x6 -> x0, local copies, waits for them, and re-layouts: 64.3 us -> none  [the longest x1 31.4 us: project_outer(): raw_outer.astype(jnp.bfloat16)]
    sub x1 -> x0, matrix products: 39.5 us -> none  [body(): attn_weights = jax.nn.softmax(affinity_matrix, axis=-1).astype(jnp.bfloat16)]
    convert_element_type x3 -> x2, other arithmetic: 19.5 us -> 1.47 us  [the longest x1 0.79 us: body(): entry.T.astype(BF16)]
  transfers between devices with their start and end apart: 6 -> 11, of which waited for: 3 -> 6; matrix products, arithmetic and copies ran while one was open for 38% -> 5% of each run, Pallas kernels for 0% -> 35%
where the time goes in v1:
time: 519 us; the launch traced here: 516 us
  waiting for transfers between devices  215 us (41%)
  Pallas kernels  208 us (40%)
  starting transfers between devices  45 us (9%)
  local copies, waits for them, and re-layouts  32.1 us (6%)
  between operations  14.1 us (3%)
    ppermute x2, waiting for transfers between devices, body(): right_oth.append(lax.ppermute(right_own[part], 'row', swap))  91.4 us
    pallas_call x3, Pallas kernels, pair_tail(): pl.pallas_call(tail_kernel, grid_spec=pltpu.PrefetchScalarGridSpec(num_sc...  77.5 us
    all_gather x1, waiting for transfers between devices, body(): bias_all = lax.all_gather(bias, 'row', axis=1, tiled=True)  70 us
    pallas_call x1, Pallas kernels, msa_block(): pl.pallas_call(functools.partial(msa_kernel, width, divisor(res, 256)), g...  49.6 us
    pallas_call x3, Pallas kernels, pair_head(): pl.pallas_call(kernel, grid=(steps,), in_specs=in_specs, out_specs=out_sp...  32 us
    all_to_all x3, waiting for transfers between devices, spread(): lax.all_to_all(values, 'row', 0, 0, tiled=True, axis_index_groups=halves)  31.9 us
    pallas_call x1, Pallas kernels, opm_block(): pl.pallas_call(opm_kernel, grid=(owned // rows,), in_specs=[pl.BlockSpec(...  31.7 us
    all_to_all x3, starting transfers between devices, collect(): lax.all_to_all(sums, 'row', 0, 0, tiled=True, axis_index_groups=halves)  18.6 us
  transfers between devices with their start and end apart: 11, of which 6 were waited for; matrix products, arithmetic and copies ran while one was open for 5% of the time, Pallas kernels for 35%

profile of v1, /device:TPU:13, one launch (start us, length us, event | category | flops | bytes accessed | tf_op | source)
XLA Modules:
  0.0 516.4 jit_solution(15865154782073965197)
XLA Ops:
  10.3 8.8 %pair_head_bias.3 = (bf16[128,16,512]{2,1,0:T(8,128)(2,1)}, bf16[8,16,512]{2,1,0:T(8,128)(2,1)}) custom-call(bf16[32,512,128]{2,1,0:T(8,128)(2,1)} %x_ref.7, f32[2,1,16]{2,1,0:T(1,128)} %bitcast.66, f32[1,512]{1,0:T(1,128)} %bitcast.62, bf16[256,128]{1,0:T(8,128)(2,1)} %get-tuple-element.19.w_ref, bf16[8,128]{1,0:T(8,128)(2,1)} %bitcast.69), custom_call_target="tpu_custom_call" | custom-call | tf_op jit(solution)/shard_map/pair_head_bias/pallas_call | solution.py:99
  19.1 4.5 all-to-all-start.1
  23.6 8.9 %pair_head_bias.2 = (bf16[128,16,512]{2,1,0:T(8,128)(2,1)}, bf16[8,16,512]{2,1,0:T(8,128)(2,1)}) custom-call(bf16[32,512,128]{2,1,0:T(8,128)(2,1)} %x_ref.7, f32[2,1,16]{2,1,0:T(1,128)} %bitcast.67, f32[1,512]{1,0:T(1,128)} %bitcast.63, bf16[256,128]{1,0:T(8,128)(2,1)} %get-tuple-element.19.w_ref, bf16[8,128]{1,0:T(8,128)(2,1)} %bitcast.70), custom_call_target="tpu_custom_call" | custom-call | tf_op jit(solution)/shard_map/pair_head_bias/pallas_call | solution.py:99
  32.5 14.8 %all-to-all-done.1.refs_1_ = bf16[8,16,16,512]{3,2,1,0:T(8,128)(2,1)S(1)} async-done(((bf16[8,16,16,512]{3,2,1,0:T(8,128)(2,1)}), bf16[8,16,16,512]{3,2,1,0:T(8,128)(2,1)S(1)}, u32[]{:S(2)}, u32[]{:S(2)}) %all-to-all-start.1) | async-done | bytes 2097184 | tf_op jit(solution)/shard_map/all_to_all | solution.py:342
  47.3 6.3 %all-to-all-start.4 = ((bf16[8,16,16,512]{3,2,1,0:T(8,128)(2,1)}), bf16[8,16,16,512]{3,2,1,0:T(8,128)(2,1)}, u32[]{:S(2)}, u32[]{:S(2)}) async-start(bf16[8,16,16,512]{3,2,1,0:T(8,128)(2,1)} %bitcast.57), calls=%async_computation.4 | async-start | bytes 4194304 | tf_op jit(solution)/shard_map/all_to_all | solution.py:342
  54.4 14.3 %pair_head.1 = bf16[128,32,512]{2,1,0:T(8,128)(2,1)} custom-call(bf16[32,512,128]{2,1,0:T(8,128)(2,1)} %x_ref.7, f32[2,1,16]{2,1,0:T(1,128)} %bitcast.68, f32[1,512]{1,0:T(1,128)} %bitcast.64, bf16[256,128]{1,0:T(8,128)(2,1)} %get-tuple-element.18.w_ref), custom_call_target="tpu_custom_call" | custom-call | tf_op jit(solution)/shard_map/pair_head/pallas_call | solution.py:99
  68.6 17.1 %all-to-all-done.4.refs_0_ = bf16[8,16,16,512]{3,2,1,0:T(8,128)(2,1)} async-done(((bf16[8,16,16,512]{3,2,1,0:T(8,128)(2,1)}), bf16[8,16,16,512]{3,2,1,0:T(8,128)(2,1)}, u32[]{:S(2)}, u32[]{:S(2)}) %all-to-all-start.4) | async-done | bytes 2097184 | tf_op jit(solution)/shard_map/all_to_all | solution.py:342
  85.8 6.7 %all-to-all-start = ((bf16[8,16,32,512]{3,2,1,0:T(8,128)(2,1)}), bf16[8,16,32,512]{3,2,1,0:T(8,128)(2,1)}, u32[]{:S(2)}, u32[]{:S(2)}) async-start(bf16[8,16,32,512]{3,2,1,0:T(8,128)(2,1)} %bitcast.50), calls=%async_computation | async-start | bytes 8388608 | tf_op jit(solution)/shard_map/all_to_all | solution.py:342
  92.4 2.3 collective-permute-start.1
  96.5 70.0 %all-gather.3.cloned.1.call-done.bias_ref = bf16[8,512,512]{2,1,0:T(8,128)(2,1)} async-done(((bf16[8,32,512]{2,1,0:T(8,128)(2,1)}), bf16[8,512,512]{2,1,0:T(8,128)(2,1)}) %all-gather.3.cloned.1.call-update) | async-done | bytes 4194320 | tf_op jit(solution)/shard_map/all_gather | solution.py:355
  166.5 49.6 %msa_block.1 = (bf16[8,512,256]{2,1,0:T(8,128)(2,1)}, bf16[8,32,512]{2,1,0:T(8,128)(2,1)}, bf16[8,32,512]{2,1,0:T(8,128)(2,1)}) custom-call(bf16[8,512,256]{2,1,0:T(8,128)(2,1)} %x_ref.6, f32[8,1,512]{2,1,0:T(1,128)} %copy.39.valid_ref, bf16[8,512,512]{2,1,0:T(8,128)(2,1)} %all-gather.3.cloned.1.call-done.bias_ref, bf16[256,1024]{1,0:T(8,128)(2,1)} %w_ref.1, ...), custom_call_target="tpu_custom_call" | custom-call | tf_op jit(solution)/shard_map/msa_block/pallas_call | solution.py:154
  216.1 1.7 copy.41
  217.9 1.7 reshape.74
  219.6 5.1 all-to-all-start.3
  224.7 1.3 copy-done.4
  226.0 5.1 tri_sums.4
  231.1 8.4 %all-to-all-done.3 = bf16[16,2,4096]{2,1,0:T(2,128)(2,1)S(1)} async-done(((bf16[16,2,4096]{2,1,0:T(2,128)(2,1)}), bf16[16,2,4096]{2,1,0:T(2,128)(2,1)S(1)}, u32[]{:S(2)}, u32[]{:S(2)}) %all-to-all-start.3) | async-done | bytes 262176 | tf_op jit(solution)/shard_map/all_to_all | solution.py:378
  240.1 3.9 all-to-all-start.5
  244.1 6.8 %tri_sums.5 = bf16[8,16,32,256]{3,2,1,0:T(8,128)(2,1)} custom-call(bf16[8,16,32,512]{3,2,1,0:T(8,128)(2,1)} %all-to-all-done.l_ref, bf16[8,16,16,512]{3,2,1,0:T(8,128)(2,1)} %all-to-all-done.4.refs_0_, bf16[8,16,16,512]{3,2,1,0:T(8,128)(2,1)} %copy-done), custom_call_target="tpu_custom_call" | custom-call | tf_op jit(solution)/shard_map/tri_sums/pallas_call | solution.py:199
  250.9 13.5 %all-to-all-done.5 = bf16[8,16,32,128]{3,2,1,0:T(8,128)(2,1)S(1)} async-done(((bf16[8,16,32,128]{3,2,1,0:T(8,128)(2,1)}), bf16[8,16,32,128]{3,2,1,0:T(8,128)(2,1)S(1)}, u32[]{:S(2)}, u32[]{:S(2)}) %all-to-all-start.5) | async-done | bytes 1048608 | tf_op jit(solution)/shard_map/all_to_all | solution.py:368
  264.3 6.9 %all-to-all-start.6 = ((bf16[8,16,32,256]{3,2,1,0:T(8,128)(2,1)}), bf16[8,16,32,256]{3,2,1,0:T(8,128)(2,1)}, u32[]{:S(2)}, u32[]{:S(2)}) async-start(bf16[8,16,32,256]{3,2,1,0:T(8,128)(2,1)} %tri_sums.5), calls=%async_computation.6 | async-start | bytes 4194304 | tf_op jit(solution)/shard_map/all_to_all | solution.py:368
  271.3 1.5 collective-permute-start
  272.8 91.4 %collective-permute-done.refs_0_ = bf16[8,16,16,512]{3,2,1,0:T(8,128)(2,1)} collective-permute-done((bf16[8,16,16,512]{3,2,1,0:T(8,128)(2,1)S(1)}, bf16[8,16,16,512]{3,2,1,0:T(8,128)(2,1)}, u32[]{:S(2)}, u32[]{:S(2)}) %collective-permute-start) | collective-permute-done | bytes 2097184 | tf_op jit(solution)/shard_map/ppermute | solution.py:352
  364.2 5.2 %tri_sums.3 = bf16[8,16,32,128]{3,2,1,0:T(8,128)(2,1)} custom-call(bf16[8,16,32,512]{3,2,1,0:T(8,128)(2,1)} %all-to-all-done.l_ref, bf16[8,16,16,512]{3,2,1,0:T(8,128)(2,1)} %collective-permute-done.refs_0_), custom_call_target="tpu_custom_call" | custom-call | tf_op jit(solution)/shard_map/tri_sums/pallas_call | solution.py:199
  369.4 7.8 %all-to-all-start.2 = ((bf16[8,16,32,128]{3,2,1,0:T(8,128)(2,1)}), bf16[8,16,32,128]{3,2,1,0:T(8,128)(2,1)S(1)}, u32[]{:S(2)}, u32[]{:S(2)}) async-start(bf16[8,16,32,128]{3,2,1,0:T(8,128)(2,1)} %tri_sums.3), calls=%async_computation.2 | async-start | bytes 2097152 | tf_op jit(solution)/shard_map/all_to_all | solution.py:368
  377.2 1.4 slice.12.wg_ref
  382.0 9.1 %copy.43 = bf16[32,128,512]{1,0,2:T(8,128)(2,1)} copy(bf16[32,128,512]{2,0,1:T(8,128)(2,1)} %all-gather.5.cloned.1.call-done) | data formatting | bytes 8388608 | tf_op jit(solution)/shard_map/all_gather | solution.py:379
  391.1 8.4 %copy.50 = bf16[64,8,32,128]{3,1,2,0:T(8,128)(2,1)} copy(bf16[64,8,32,128]{3,2,1,0:T(8,128)(2,1)} %bitcast.51) | data formatting | bytes 8388608
  399.4 31.7 %opm_block.1 = f32[32,512,128]{2,1,0:T(8,128)} custom-call(bf16[32,128,32]{2,1,0:T(8,128)(2,1)} %bitcast.54, bf16[512,4096]{1,0:T(8,128)(2,1)} %bitcast.49, bf16[32,4096]{1,0:T(8,128)(2,1)} %reshape.67.w_ref, bf16[512,128]{1,0:T(8,128)(2,1)} %get-tuple-element.16.vt_ref, f32[4,128,8]{2,1,0:T(8,128)} %bitcast.59), custom_call_target="tpu_custom_call" | custom-call | tf_op jit(solution)/shard_map/opm_block/pallas_call | solution.py:232
  431.1 37.7 %pair_tail.3.refs_0_ = bf16[32,16,2,16,128]{4,3,2,1,0:T(8,128)(2,1)} custom-call(s32[1]{0:T(128)} %bitcast.6.half_ref, bf16[32,16,2,16,128]{4,3,2,1,0:T(8,128)(2,1)} %bitcast.42, bf16[128,32,256]{2,1,0:T(8,128)(2,1)} %bitcast.23.tri_ref, f32[32,16,2,16,128]{4,3,2,1,0:T(8,128)} %bitcast.45, bf16[128,128]{1,0:T(8,128)(2,1)} %slice.12.wg_ref, ...), custom_call_target="tpu_custom_call" | custom-call | tf_op jit(solution)/shard_map/pair_tail/pallas_call | solution.py:291
  468.8 19.9 %pair_tail.4.refs_0_ = bf16[32,16,2,16,128]{4,3,2,1,0:T(8,128)(2,1)} custom-call(s32[1]{0:T(128)S(6)} %sub.9.half_ref, bf16[32,16,2,16,128]{4,3,2,1,0:T(8,128)(2,1)} %bitcast.43, bf16[128,32,128]{2,1,0:T(8,128)(2,1)} %bitcast.52, f32[32,16,2,16,128]{4,3,2,1,0:T(8,128)} %bitcast.46, bf16[128,128]{1,0:T(8,128)(2,1)} %slice.12.wg_ref, ...), custom_call_target="tpu_custom_call", output_to_operand_aliasing={{}: (8, {})} | custom-call | tf_op jit(solution)/shard_map/pair_tail/pallas_call | solution.py:291
  489.7 19.9 %pair_tail.5 = bf16[32,16,2,16,128]{4,3,2,1,0:T(8,128)(2,1)} custom-call(s32[1]{0:T(128)S(6)} %sub.9.half_ref, bf16[32,16,2,16,128]{4,3,2,1,0:T(8,128)(2,1)} %bitcast.44, bf16[128,32,128]{2,1,0:T(8,128)(2,1)} %bitcast.53, f32[32,16,2,16,128]{4,3,2,1,0:T(8,128)} %bitcast.47, bf16[128,128]{1,0:T(8,128)(2,1)} %slice.12.wg_ref, ...), custom_call_target="tpu_custom_call", output_to_operand_aliasing={{}: (8, {})} | custom-call | tf_op jit(solution)/shard_map/pair_tail/pallas_call | solution.py:291
  (49 shorter events, 10.8 us)
Async XLA Ops:
  7.9 2.5 copy-start.11
  19.1 28.2 %all-to-all-start.1 = ((bf16[8,16,16,512]{3,2,1,0:T(8,128)(2,1)}), bf16[8,16,16,512]{3,2,1,0:T(8,128)(2,1)S(1)}, u32[]{:S(2)}, u32[]{:S(2)}) async-start(bf16[8,16,16,512]{3,2,1,0:T(8,128)(2,1)} %bitcast.58), calls=%async_computation.1 | async-start | bytes 4194304 | tf_op jit(solution)/shard_map/all_to_all | solution.py:342
  23.6 30.0 %copy-start.9 = (bf16[8,16,512]{2,1,0:T(8,128)(2,1)S(1)}, bf16[8,16,512]{2,1,0:T(8,128)(2,1)}, u32[]{:S(2)}) copy-start(bf16[8,16,512]{2,1,0:T(8,128)(2,1)} %get-tuple-element.10) | copy-start | bytes 393220
  32.5 21.1 %copy-start.10 = (bf16[8,16,512]{2,1,0:T(8,128)(2,1)S(1)}, bf16[8,16,512]{2,1,0:T(8,128)(2,1)}, u32[]{:S(2)}) copy-start(bf16[8,16,512]{2,1,0:T(8,128)(2,1)} %get-tuple-element.9) | copy-start | bytes 393220
  47.3 21.4 %copy-start = (bf16[8,16,16,512]{3,2,1,0:T(8,128)(2,1)}, bf16[8,16,16,512]{3,2,1,0:T(8,128)(2,1)S(1)}, u32[]{:S(2)}) copy-start(bf16[8,16,16,512]{3,2,1,0:T(8,128)(2,1)S(1)} %all-to-all-done.1.refs_1_) | copy-start | bytes 6291460
  47.3 38.5 %all-to-all-start.4 = ((bf16[8,16,16,512]{3,2,1,0:T(8,128)(2,1)}), bf16[8,16,16,512]{3,2,1,0:T(8,128)(2,1)}, u32[]{:S(2)}, u32[]{:S(2)}) async-start(bf16[8,16,16,512]{3,2,1,0:T(8,128)(2,1)} %bitcast.57), calls=%async_computation.4 | async-start | bytes 4194304 | tf_op jit(solution)/shard_map/all_to_all | solution.py:342
  53.6 112.9 %all-gather.3.cloned.1.call-start = ((), (), s32[]{:S(2)}) async-start(), calls=%async_computation.7 | async-start | bytes 4456448 | tf_op jit(solution)/shard_map/all_gather | solution.py:355
  85.8 9.0 %copy-start.7 = (s32[128,512]{1,0:T(8,128)S(1)}, s32[128,512]{1,0:T(8,128)}, u32[]{:S(2)}) copy-start(s32[128,512]{1,0:T(8,128)} %param.15) | copy-start | bytes 786436
  85.8 9.1 %copy-start.12 = (f32[512]{0:T(512)S(1)}, f32[512]{0:T(512)}, u32[]{:S(2)}) copy-start(f32[512]{0:T(512)} %copy-done.11) | copy-start | bytes 6148
  85.8 133.8 %all-to-all-start = ((bf16[8,16,32,512]{3,2,1,0:T(8,128)(2,1)}), bf16[8,16,32,512]{3,2,1,0:T(8,128)(2,1)}, u32[]{:S(2)}, u32[]{:S(2)}) async-start(bf16[8,16,32,512]{3,2,1,0:T(8,128)(2,1)} %bitcast.50), calls=%async_computation | async-start | bytes 8388608 | tf_op jit(solution)/shard_map/all_to_all | solution.py:342
  92.4 289.5 %all-gather.5.cloned.1.call-start = ((), (), s32[]{:S(2)}) async-start(), calls=%async_computation.8 | async-start | bytes 4456448 | tf_op jit(solution)/shard_map/all_gather | solution.py:379
  92.4 132.2 %collective-permute-start.1 = (bf16[8,16,16,512]{3,2,1,0:T(8,128)(2,1)}, bf16[8,16,16,512]{3,2,1,0:T(8,128)(2,1)S(1)}, u32[]{:S(2)}, u32[]{:S(2)}) collective-permute-start(bf16[8,16,16,512]{3,2,1,0:T(8,128)(2,1)} %all-to-all-done.4.refs_0_), channel_id=1, source_target_pairs={{0,8},{1,9},{2,10},{3,11},{4,12},{5,13},{6,14},{7,15},{8,0},{9,1},... | collective-permute-start | bytes 6291464 | tf_op jit(solution)/shard_map/ppermute | solution.py:352
  219.6 19.9 %all-to-all-start.3 = ((bf16[16,2,4096]{2,1,0:T(2,128)(2,1)}), bf16[16,2,4096]{2,1,0:T(2,128)(2,1)S(1)}, u32[]{:S(2)}, u32[]{:S(2)}) async-start(bf16[16,2,4096]{2,1,0:T(2,128)(2,1)} %reshape.74), calls=%async_computation.3 | async-start | bytes 524288 | tf_op jit(solution)/shard_map/all_to_all | solution.py:378
  224.7 1.3 copy-start.4
  239.4 0.7 copy-start.5
  240.1 24.2 %all-to-all-start.5 = ((bf16[8,16,32,128]{3,2,1,0:T(8,128)(2,1)}), bf16[8,16,32,128]{3,2,1,0:T(8,128)(2,1)S(1)}, u32[]{:S(2)}, u32[]{:S(2)}) async-start(bf16[8,16,32,128]{3,2,1,0:T(8,128)(2,1)} %tri_sums.4), calls=%async_computation.5 | async-start | bytes 2097152 | tf_op jit(solution)/shard_map/all_to_all | solution.py:368
  250.9 20.4 %copy-start.1 = (bf16[8,16,16,512]{3,2,1,0:T(8,128)(2,1)S(1)}, bf16[8,16,16,512]{3,2,1,0:T(8,128)(2,1)}, u32[]{:S(2)}) copy-start(bf16[8,16,16,512]{3,2,1,0:T(8,128)(2,1)} %copy-done) | copy-start | bytes 6291460
  264.3 105.1 %copy-start.2 = (bf16[8,16,32,128]{3,2,1,0:T(8,128)(2,1)}, bf16[8,16,32,128]{3,2,1,0:T(8,128)(2,1)S(1)}, u32[]{:S(2)}) copy-start(bf16[8,16,32,128]{3,2,1,0:T(8,128)(2,1)S(1)} %all-to-all-done.5) | copy-start | bytes 3145732
  264.3 105.1 %all-to-all-start.6 = ((bf16[8,16,32,256]{3,2,1,0:T(8,128)(2,1)}), bf16[8,16,32,256]{3,2,1,0:T(8,128)(2,1)}, u32[]{:S(2)}, u32[]{:S(2)}) async-start(bf16[8,16,32,256]{3,2,1,0:T(8,128)(2,1)} %tri_sums.5), calls=%async_computation.6 | async-start | bytes 4194304 | tf_op jit(solution)/shard_map/all_to_all | solution.py:368
  271.3 92.9 %collective-permute-start = (bf16[8,16,16,512]{3,2,1,0:T(8,128)(2,1)S(1)}, bf16[8,16,16,512]{3,2,1,0:T(8,128)(2,1)}, u32[]{:S(2)}, u32[]{:S(2)}) collective-permute-start(bf16[8,16,16,512]{3,2,1,0:T(8,128)(2,1)S(1)} %copy-done.1), channel_id=1, source_target_pairs={{0,8},{1,9},{2,10},{3,11},{4,12},{5,13},{6,14},{7,15},{8,0},{9,1},... | collective-permute-start | bytes 6291464 | tf_op jit(solution)/shard_map/ppermute | solution.py:352
  364.2 14.3 %copy-start.8 = (bf16[1024,128]{1,0:T(8,128)(2,1)S(1)}, bf16[1024,128]{1,0:T(8,128)(2,1)}, u32[]{:S(2)}) copy-start(bf16[1024,128]{1,0:T(8,128)(2,1)} %param.21) | copy-start | bytes 786436
  364.2 16.0 %copy-start.6 = (bf16[16,2,4096]{2,1,0:T(2,128)(2,1)S(1)}, bf16[16,2,4096]{2,1,0:T(2,128)(2,1)}, u32[]{:S(2)}) copy-start(bf16[16,2,4096]{2,1,0:T(2,128)(2,1)} %copy-done.5) | copy-start | bytes 786436
  369.4 119.3 %all-to-all-start.2 = ((bf16[8,16,32,128]{3,2,1,0:T(8,128)(2,1)}), bf16[8,16,32,128]{3,2,1,0:T(8,128)(2,1)S(1)}, u32[]{:S(2)}, u32[]{:S(2)}) async-start(bf16[8,16,32,128]{3,2,1,0:T(8,128)(2,1)} %tri_sums.3), calls=%async_computation.2 | async-start | bytes 2097152 | tf_op jit(solution)/shard_map/all_to_all | solution.py:368
  488.7 1.0 copy-start.3
Sparse Core Ops, SparseCore 0:
  57.1 109.3 all-gather.2
  216.3 82.4 all-gather.4

commit v2 on v1

--- a/solution.py
+++ b/solution.py
@@ -13,7 +13,8 @@
 BF16 = jnp.bfloat16
 LANES = 128
 HEAD_UNROLL = 4
-TAIL_UNROLL = 4
+TAIL_UNROLL = 2
+TAIL_ROWS = 8
 
 
 def norm(values, axis=-1):
@@ -107,7 +108,7 @@
     )(*args)
 
 
-def msa_kernel(width, chunk, x_ref, valid_ref, bias_ref, w_ref, wf_ref, wp_ref, o_ref, l_ref, r_ref, q_s, k_s, v_s, att):
+def msa_kernel(width, chunk, order, x_ref, valid_ref, bias_ref, w_ref, wf_ref, wp_ref, o_ref, l_ref, r_ref, q_s, k_s, v_s, att):
     res, feat = x_ref.shape[1:]
     half = feat // 2
     per_half = half // width
@@ -128,7 +129,10 @@
             for c in range(res // chunk):
                 span = slice(c * chunk, (c + 1) * chunk)
                 q = jnp.where(mine, q_s[span], jnp.zeros((), BF16))
-                s = dot(q, k_s[...], 1, 1) + bias_ref[step + side * per_half, span].astype(F32)
+                lines = bias_ref.shape[2]
+                owners = order[c * chunk // lines : (c + 1) * chunk // lines]
+                bias = jnp.concatenate([bias_ref[g, step + side * per_half] for g in owners], axis=0)
+                s = dot(q, k_s[...], 1, 1) + bias.astype(F32)
                 s = jnp.where(valid > 0, s, -1000000000.0)
                 p = jnp.exp(s - jnp.max(s, axis=1, keepdims=True)).astype(BF16)
                 out = dot(p, v)
@@ -148,11 +152,11 @@
     r_ref[0] = factors[outer : 2 * outer].astype(BF16)
 
 
-def msa_block(x, valid, bias, w, wf, wp, width):
+def msa_block(x, valid, bias, order, w, wf, wp, width):
     seqs, res, feat = x.shape
     outer = wp.shape[0] // 2
     return pl.pallas_call(
-        functools.partial(msa_kernel, width, divisor(res, 256)),
+        functools.partial(msa_kernel, width, divisor(res, 256), order),
         grid=(seqs,),
         in_specs=[
             pl.BlockSpec((1, res, feat), lambda s: (s, 0, 0)),
@@ -206,29 +210,44 @@
     )(left, *rights)
 
 
-def opm_kernel(l_ref, r_ref, w_ref, vt_ref, vi_ref, o_ref, mix):
+def opm_kernel(l_ref, r_ref, w_ref, vt_ref, vi_ref, two_ref, o_ref, sum_ref, mix, right):
     rows, seqs, outer = l_ref.shape
+    owners, inner, local, res = r_ref.shape
     cz = o_ref.shape[2]
-    inner = w_ref.shape[1] // cz
+    depth = inner * local
+
+    @pl.when(pl.program_id(0) == 0)
+    def _():
+        for g in range(owners):
+            right[:, g * depth : (g + 1) * depth] = r_ref[g].reshape(depth, res).T
+
+    many = max(16 // local, 1)
     for first in range(0, rows, 2):
         pair = min(2, rows - first)
         both = l_ref[first : first + pair].reshape(pair * seqs, outer)
-        for d in range(inner):
-            part = dot(both, w_ref[:, d * cz : (d + 1) * cz]).astype(BF16)
+        for d in range(0, inner, many):
+            made = [dot(both, w_ref[:, (d + m) * cz : (d + m + 1) * cz]) for m in range(many)]
             for n in range(pair):
-                mix[d * seqs : (d + 1) * seqs, n * cz : (n + 1) * cz] = part[n * seqs : (n + 1) * seqs]
-        total = dot(r_ref[...], mix[:, 0 : pair * cz])
+                for g in range(owners):
+                    at = n * seqs + g * local
+                    lines = jnp.concatenate([t[at : at + local] for t in made], axis=0).astype(BF16)
+                    to = g * depth + d * local
+                    mix[to : to + many * local, n * cz : (n + 1) * cz] = lines
+        total = dot(right[...], mix[:, 0 : pair * cz])
         for n in range(pair):
             mine = jnp.broadcast_to(vi_ref[:, first + n : first + n + 1], (seqs, cz)).astype(BF16)
             tally = jnp.maximum(dot(vt_ref[...], mine), 1.0)
-            o_ref[first + n] = total[:, n * cz : (n + 1) * cz] / tally
-
-
-def opm_block(left, right, w, valid_t, mine):
+            mean = total[:, n * cz : (n + 1) * cz] / tally
+            o_ref[first + n] = mean
+            sum_ref[first + n] = (mean + two_ref[first + n]).astype(BF16)
+
+
+def opm_block(left, right, w, valid_t, mine, two):
     owned, seqs, outer = left.shape
-    res, depth = right.shape
-    cz = w.shape[1] // (depth // seqs)
+    _, inner, _, res = right.shape
+    cz = w.shape[1] // inner
     rows = divisor(owned, 8)
+    pair = pl.BlockSpec((rows, res, cz), lambda g: (g, 0, 0))
     return pl.pallas_call(
         opm_kernel,
         grid=(owned // rows,),
@@ -238,58 +257,66 @@
             full(w.shape),
             full(valid_t.shape),
             pl.BlockSpec((None, seqs, rows), lambda g: (g, 0, 0)),
+            pair,
         ],
-        out_specs=pl.BlockSpec((rows, res, cz), lambda g: (g, 0, 0)),
-        out_shape=jax.ShapeDtypeStruct((owned, res, cz), F32),
-        scratch_shapes=[pltpu.VMEM((depth, 2 * cz), BF16)],
+        out_specs=[pair, pair],
+        out_shape=[
+            jax.ShapeDtypeStruct((owned, res, cz), F32),
+            jax.ShapeDtypeStruct((owned, res, cz), BF16),
+        ],
+        scratch_shapes=[pltpu.VMEM((seqs * inner, 2 * cz), BF16), pltpu.VMEM((res, seqs * inner), BF16)],
         name="opm_block",
-    )(left, right, w, valid_t, mine.reshape(seqs, owned // rows, rows).transpose(1, 0, 2))
-
-
-def tail_kernel(half_ref, x_ref, tri_ref, opm_ref, wg_ref, wt_ref, w1_ref, w2_ref, *refs):
+    )(left, right, w, valid_t, mine.reshape(seqs, owned // rows, rows).transpose(1, 0, 2), two)
+
+
+def tail_kernel(last, half_ref, x_ref, tri_ref, wg_ref, wt_ref, w1_ref, w2_ref, *refs):
+    opm_ref = refs[0]
     o_ref, scr = refs[-2:]
     rows, groups, lines, cz = x_ref.shape
+    cols = groups * lines
+    many = divisor(rows, TAIL_ROWS)
     for n in range(scr.shape[0]):
         part = tri_ref[:, :, n * LANES : (n + 1) * LANES]
         scr[n] = part.astype(F32).reshape(scr.shape[1:])
 
-    def row(i, carry):
-        x = x_ref[i].reshape(groups * lines, cz).astype(F32)
+    def block(b, carry):
+        i = b * many
+        x = x_ref[pl.ds(i, many)].reshape(many * cols, cz).astype(F32)
         gate = jax.nn.sigmoid(dot(norm(x).astype(BF16), wg_ref[...]))
-        tri = norm(get_rows(scr, i, rows), 0).astype(BF16)
-        one = x + gate * dot(tri, wt_ref[...], 0, 0)
+        tri = [dot(norm(get_rows(scr, i + m, rows), 0).astype(BF16), wt_ref[...], 0, 0) for m in range(many)]
+        one = x + gate * jnp.concatenate(tri, axis=0)
         hidden = jnp.maximum(dot(norm(one).astype(BF16), w1_ref[...]), 0.0).astype(BF16)
-        out = one + dot(hidden, w2_ref[...]) + opm_ref[i].reshape(groups * lines, cz)
-        o_ref[i] = out.astype(BF16).reshape(groups, lines, cz)
+        out = one + dot(hidden, w2_ref[...])
+        if last:
+            out = out + opm_ref[pl.ds(i, many)].reshape(many * cols, cz)
+        o_ref[pl.ds(i, many)] = out.astype(o_ref.dtype).reshape(many, groups, lines, cz)
         return carry
 
-    lax.fori_loop(0, rows, row, 0, unroll=TAIL_UNROLL)
-
-
-def pair_tail(half, first, parts, x, tri, opm, wg, wt, w1, w2, earlier=None):
+    lax.fori_loop(0, rows // many, block, 0, unroll=TAIL_UNROLL)
+
+
+def pair_tail(half, first, parts, x, tri, weights, opm=None, earlier=None):
     owned, res, cz = x.shape
     ring = res // owned
     rows = divisor(owned, 16)
     lines = owned // parts
     span = ring // 2 * lines
     count = tri.shape[2] // span
+    last = opm is not None
     view = (owned, ring, parts, lines, cz)
     pair = pl.BlockSpec((rows, ring // 2, None, lines, cz), lambda q, g, h: (g, h[0], first + q, 0, 0))
-    in_specs = [
-        pair,
-        pl.BlockSpec((cz, rows, span), lambda q, g, h: (0, g, q)),
-        pair,
-        full(wg.shape),
-        full(wt.shape),
-        full(w1.shape),
-        full(w2.shape),
-    ]
-    args = [half, x.reshape(view), tri, opm.reshape(view), wg, wt, w1, w2]
+    in_specs = [pair, pl.BlockSpec((cz, rows, span), lambda q, g, h: (0, g, q))] + [full(w.shape) for w in weights]
+    args = [half, x.reshape(view), tri, *weights]
+    if last:
+        in_specs.append(pair)
+        args.append(opm.reshape(view))
+    aliases = {}
     if earlier is not None:
+        aliases = {len(args): 0}
         in_specs.append(pl.BlockSpec(memory_space=pl.ANY))
         args.append(earlier.reshape(view))
     return pl.pallas_call(
-        tail_kernel,
+        functools.partial(tail_kernel, last),
         grid_spec=pltpu.PrefetchScalarGridSpec(
             num_scalar_prefetch=1,
             grid=(count, owned // rows),
@@ -297,9 +324,9 @@
             out_specs=pair,
             scratch_shapes=[pltpu.VMEM((max(span // LANES, 1), cz * rows, min(span, LANES)), F32)],
         ),
-        out_shape=jax.ShapeDtypeStruct(view, BF16),
-        input_output_aliases={} if earlier is None else {8: 0},
-        name="pair_tail",
+        out_shape=jax.ShapeDtypeStruct(view, BF16 if last else F32),
+        input_output_aliases=aliases,
+        name="pair_tail_last" if last else "pair_tail",
     )(*args).reshape(owned, res, cz)
 
 
@@ -352,12 +379,24 @@
         right_oth.append(lax.ppermute(right_own[part], "row", swap))
     (left,) = pair_head(coupling_features, my_residue, residue, trio[0 : 2 * cz])
     left_own = spread(left)
-    bias_all = lax.all_gather(bias, "row", axis=1, tiled=True)
+    planes = 4 if ring % 4 == 0 else 1
+    members = ring // planes
+    across = [[m + members * z for z in range(planes)] for m in range(members)]
+    within = [[m + members * z for m in range(members)] for z in range(planes)]
+    order = [m * planes + z for z in range(planes) for m in range(members)]
+
+    def gather(values):
+        values = lax.all_gather(values, "row", axis=0, axis_index_groups=across)
+        values = lax.all_gather(values, "row", axis=0, axis_index_groups=within)
+        return values.reshape((ring,) + values.shape[2:])
+
+    bias_all = gather(bias)
 
     msa_out, left_opm, right_opm = msa_block(
         aligned_features,
         my_entry,
         bias_all,
+        order,
         lookup_matrices,
         aligned_final_matrix,
         product_factor_matrices.T,
@@ -375,15 +414,27 @@
         sums = tri_sums(left_own, [right_oth[part]])
         tri_oth.append(collect(sums))
 
+    right_all = gather(right_opm.transpose(1, 0, 2))
     left_res = lax.all_to_all(left_opm, "row", split_axis=2, concat_axis=0, tiled=True).transpose(2, 0, 1)
-    right_all = lax.all_gather(right_opm.transpose(1, 0, 2), "row", axis=1, tiled=True)
-    right_all = right_all.reshape(outer * ring * seqs, res).T
-    mine = lax.dynamic_slice_in_dim(entry, place * owned, owned, 1)
-    opm = opm_block(left_res, right_all, product_final_matrix.reshape(outer, outer * cz), entry.T.astype(BF16), mine)
+    left_res = left_res.reshape(owned, planes, members, seqs, outer).transpose(0, 2, 1, 3, 4)
+    left_res = left_res.reshape(owned, ring * seqs, outer)
+    entry_order = entry.reshape(planes, members, seqs, res).transpose(1, 0, 2, 3).reshape(ring * seqs, res)
+    mine = lax.dynamic_slice_in_dim(entry_order, place * owned, owned, 1)
     weights = (trio_factor_matrices[:, 4 * cz : 5 * cz], trio_final_matrix, feedforward_expand, feedforward_shrink)
-    pair = pair_tail(half, 0, parts, coupling_features, tri_own, opm, *weights)
-    for part in range(parts):
-        pair = pair_tail(1 - half, part, parts, coupling_features, tri_oth[part], opm, *weights, earlier=pair)
+    two = pair_tail(half, 0, parts, coupling_features, tri_own, weights)
+    for part in range(parts - 1):
+        two = pair_tail(1 - half, part, parts, coupling_features, tri_oth[part], weights, earlier=two)
+    opm, pair = opm_block(
+        left_res,
+        right_all,
+        product_final_matrix.reshape(outer, outer * cz),
+        entry_order.T.astype(BF16),
+        mine,
+        two,
+    )
+    pair = pair_tail(
+        1 - half, parts - 1, parts, coupling_features, tri_oth[-1], weights, opm=opm, earlier=pair
+    )
     return (msa_out, pair)
 
 

time: 519 us -> 456 us (0.88)
  Pallas kernels: 208 us -> 167 us
  local copies, waits for them, and re-layouts: 32.1 us -> 18.2 us
    pallas_call x4, Pallas kernels: 127 us -> 82.3 us  [the longest x1 50.3 us: msa_block(): pl.pallas_call(functools.partial(msa_kernel, width, divisor(res, 256), or...]
    all_to_all x3, waiting for transfers between devices: 13.5 us -> 1.97 us  [collect(): lax.all_to_all(sums, 'row', 0, 0, tiled=True, axis_index_groups=halves)]
    unnamed x31 -> x29, local copies, waits for them, and re-layouts: 14.8 us -> 6.29 us
    all_to_all x3, waiting for transfers between devices: 31.9 us -> 38.3 us  [spread(): lax.all_to_all(values, 'row', 0, 0, tiled=True, axis_index_groups=halves)]
    all_gather x1, local copies, waits for them, and re-layouts: 9.11 us -> 2.81 us  [gather(): values = lax.all_gather(values, 'row', axis=0, axis_index_groups=across)]
    all_gather x2 -> x4, waiting for transfers between devices: 70 us -> 71.6 us  [the longest x2 68.8 us: gather(): values = lax.all_gather(values, 'row', axis=0, axis_index_groups=within)]
  transfers between devices with their start and end apart: 11 -> 13, of which waited for: 6 -> 7; matrix products, arithmetic and copies ran while one was open for 5% -> 3% of each run, Pallas kernels for 35% -> 33%
where the time goes in v2:
time: 456 us; the launch traced here: 454 us
  waiting for transfers between devices  211 us (46%)
  Pallas kernels  167 us (37%)
  starting transfers between devices  42.5 us (9%)
  local copies, waits for them, and re-layouts  18.2 us (4%)
  between operations  13.8 us (3%)
    ppermute x2, waiting for transfers between devices, body(): right_oth.append(lax.ppermute(right_own[part], 'row', swap))  89.6 us
    all_gather x2, waiting for transfers between devices, gather(): values = lax.all_gather(values, 'row', axis=0, axis_index_groups=within)  68.8 us
    pallas_call x1, Pallas kernels, msa_block(): pl.pallas_call(functools.partial(msa_kernel, width, divisor(res, 256), or...  50.3 us
    all_to_all x3, waiting for transfers between devices, spread(): lax.all_to_all(values, 'row', 0, 0, tiled=True, axis_index_groups=halves)  38.3 us
    pallas_call x1, Pallas kernels, opm_block(): pl.pallas_call(opm_kernel, grid=(owned // rows,), in_specs=[pl.BlockSpec(...  35.8 us
    pallas_call x3, Pallas kernels, pair_tail(): pl.pallas_call(functools.partial(tail_kernel, last), grid_spec=pltpu.Pref...  32 us
    pallas_call x3, Pallas kernels, pair_head(): pl.pallas_call(kernel, grid=(steps,), in_specs=in_specs, out_specs=out_sp...  31.9 us
    all_to_all x3, starting transfers between devices, spread(): lax.all_to_all(values, 'row', 0, 0, tiled=True, axis_index_groups=halves)  19.5 us
  transfers between devices with their start and end apart: 13, of which 7 were waited for; matrix products, arithmetic and copies ran while one was open for 3% of the time, Pallas kernels for 33%

profile of v2, /device:TPU:13, one launch (start us, length us, event | category | flops | bytes accessed | tf_op | source)
XLA Modules:
  0.0 454.1 jit_solution(16122947462688394238)
XLA Ops:
  8.6 1.1 copy.46
  10.3 8.8 %pair_head_bias.3 = (bf16[128,16,512]{2,1,0:T(8,128)(2,1)}, bf16[8,16,512]{2,1,0:T(8,128)(2,1)}) custom-call(bf16[32,512,128]{2,1,0:T(8,128)(2,1)} %x_ref.7, f32[2,1,16]{2,1,0:T(1,128)} %bitcast.73, f32[1,512]{1,0:T(1,128)} %bitcast.69, bf16[256,128]{1,0:T(8,128)(2,1)} %get-tuple-element.21.w_ref, bf16[8,128]{1,0:T(8,128)(2,1)} %bitcast.76), custom_call_target="tpu_custom_call" | custom-call | tf_op jit(solution)/shard_map/pair_head_bias/pallas_call | solution.py:100
  19.1 4.5 all-to-all-start.1
  23.6 8.9 %pair_head_bias.2 = (bf16[128,16,512]{2,1,0:T(8,128)(2,1)}, bf16[8,16,512]{2,1,0:T(8,128)(2,1)}) custom-call(bf16[32,512,128]{2,1,0:T(8,128)(2,1)} %x_ref.7, f32[2,1,16]{2,1,0:T(1,128)} %bitcast.74, f32[1,512]{1,0:T(1,128)} %bitcast.70, bf16[256,128]{1,0:T(8,128)(2,1)} %get-tuple-element.21.w_ref, bf16[8,128]{1,0:T(8,128)(2,1)} %bitcast.77), custom_call_target="tpu_custom_call" | custom-call | tf_op jit(solution)/shard_map/pair_head_bias/pallas_call | solution.py:100
  32.5 14.8 %all-to-all-done.1.refs_1_ = bf16[8,16,16,512]{3,2,1,0:T(8,128)(2,1)S(1)} async-done(((bf16[8,16,16,512]{3,2,1,0:T(8,128)(2,1)}), bf16[8,16,16,512]{3,2,1,0:T(8,128)(2,1)S(1)}, u32[]{:S(2)}, u32[]{:S(2)}) %all-to-all-start.1) | async-done | bytes 2097184 | tf_op jit(solution)/shard_map/all_to_all | solution.py:369
  47.3 6.3 %all-to-all-start.4 = ((bf16[8,16,16,512]{3,2,1,0:T(8,128)(2,1)}), bf16[8,16,16,512]{3,2,1,0:T(8,128)(2,1)}, u32[]{:S(2)}, u32[]{:S(2)}) async-start(bf16[8,16,16,512]{3,2,1,0:T(8,128)(2,1)} %bitcast.57), calls=%async_computation.4 | async-start | bytes 4194304 | tf_op jit(solution)/shard_map/all_to_all | solution.py:369
  54.4 14.3 %pair_head.1 = bf16[128,32,512]{2,1,0:T(8,128)(2,1)} custom-call(bf16[32,512,128]{2,1,0:T(8,128)(2,1)} %x_ref.7, f32[2,1,16]{2,1,0:T(1,128)} %bitcast.75, f32[1,512]{1,0:T(1,128)} %bitcast.71, bf16[256,128]{1,0:T(8,128)(2,1)} %get-tuple-element.20.w_ref), custom_call_target="tpu_custom_call" | custom-call | tf_op jit(solution)/shard_map/pair_head/pallas_call | solution.py:100
  68.6 23.5 %all-to-all-done.4.refs_0_ = bf16[8,16,16,512]{3,2,1,0:T(8,128)(2,1)} async-done(((bf16[8,16,16,512]{3,2,1,0:T(8,128)(2,1)}), bf16[8,16,16,512]{3,2,1,0:T(8,128)(2,1)}, u32[]{:S(2)}, u32[]{:S(2)}) %all-to-all-start.4) | async-done | bytes 2097184 | tf_op jit(solution)/shard_map/all_to_all | solution.py:369
  92.2 8.7 %all-to-all-start = ((bf16[8,16,32,512]{3,2,1,0:T(8,128)(2,1)}), bf16[8,16,32,512]{3,2,1,0:T(8,128)(2,1)}, u32[]{:S(2)}, u32[]{:S(2)}) async-start(bf16[8,16,32,512]{3,2,1,0:T(8,128)(2,1)} %bitcast.48), calls=%async_computation | async-start | bytes 8388608 | tf_op jit(solution)/shard_map/all_to_all | solution.py:369
  102.9 68.8 %all-gather.11.cloned.1.call-done.bias_ref = bf16[16,8,32,512]{3,2,1,0:T(8,128)(2,1)} async-done(((bf16[4,8,32,512]{3,2,1,0:T(8,128)(2,1)}), bf16[16,8,32,512]{3,2,1,0:T(8,128)(2,1)}) %all-gather.11.cloned.1.call-update) | async-done | bytes 4194320 | tf_op jit(solution)/shard_map/all_gather | solution.py:390
  171.7 50.3 %msa_block.1 = (bf16[8,512,256]{2,1,0:T(8,128)(2,1)}, bf16[8,32,512]{2,1,0:T(8,128)(2,1)}, bf16[8,32,512]{2,1,0:T(8,128)(2,1)}) custom-call(bf16[8,512,256]{2,1,0:T(8,128)(2,1)} %x_ref.6, f32[8,1,512]{2,1,0:T(1,128)} %reshape.78.valid_ref, bf16[16,8,32,512]{3,2,1,0:T(8,128)(2,1)} %all-gather.11.cloned.1.call-done.bias_ref, bf16[256,1024]{1,0:T(8,128)(2,1)} %w_ref.1, ...), custom_call_target="tpu_custom_call" | custom-call | tf_op jit(solution)/shard_map/msa_block/pallas_call | solution.py:158
  222.0 1.7 copy.50
  223.8 1.7 reshape.106
  225.5 4.1 all-to-all-start.3
  229.6 1.3 copy-done.4
  230.9 5.1 %tri_sums.4 = bf16[8,16,32,128]{3,2,1,0:T(8,128)(2,1)} custom-call(bf16[8,16,32,512]{3,2,1,0:T(8,128)(2,1)} %all-to-all-done.l_ref, bf16[8,16,16,512]{3,2,1,0:T(8,128)(2,1)} %copy-done.4), custom_call_target="tpu_custom_call" | custom-call | tf_op jit(solution)/shard_map/tri_sums/pallas_call | solution.py:203
  236.0 9.1 %all-to-all-done.3 = bf16[16,2,4096]{2,1,0:T(2,128)(2,1)S(1)} async-done(((bf16[16,2,4096]{2,1,0:T(2,128)(2,1)}), bf16[16,2,4096]{2,1,0:T(2,128)(2,1)S(1)}, u32[]{:S(2)}, u32[]{:S(2)}) %all-to-all-start.3) | async-done | bytes 262176 | tf_op jit(solution)/shard_map/all_to_all | solution.py:418
  245.9 3.9 all-to-all-start.5
  249.8 2.8 all-gather.13.cloned.1.call-done
  252.6 2.8 copy.54
  255.5 6.4 %tri_sums.5 = bf16[8,16,32,256]{3,2,1,0:T(8,128)(2,1)} custom-call(bf16[8,16,32,512]{3,2,1,0:T(8,128)(2,1)} %all-to-all-done.l_ref, bf16[8,16,16,512]{3,2,1,0:T(8,128)(2,1)} %all-to-all-done.4.refs_0_, bf16[8,16,16,512]{3,2,1,0:T(8,128)(2,1)} %copy-done), custom_call_target="tpu_custom_call" | custom-call | tf_op jit(solution)/shard_map/tri_sums/pallas_call | solution.py:203
  261.9 2.0 all-to-all-done.5
  263.9 6.4 %all-to-all-start.6 = ((bf16[8,16,32,256]{3,2,1,0:T(8,128)(2,1)}), bf16[8,16,32,256]{3,2,1,0:T(8,128)(2,1)}, u32[]{:S(2)}, u32[]{:S(2)}) async-start(bf16[8,16,32,256]{3,2,1,0:T(8,128)(2,1)} %tri_sums.5), calls=%async_computation.6 | async-start | bytes 4194304 | tf_op jit(solution)/shard_map/all_to_all | solution.py:407
  271.2 89.6 %collective-permute-done.refs_0_ = bf16[8,16,16,512]{3,2,1,0:T(8,128)(2,1)} collective-permute-done((bf16[8,16,16,512]{3,2,1,0:T(8,128)(2,1)S(1)}, bf16[8,16,16,512]{3,2,1,0:T(8,128)(2,1)}, u32[]{:S(2)}, u32[]{:S(2)}) %collective-permute-start) | collective-permute-done | bytes 2097184 | tf_op jit(solution)/shard_map/ppermute | solution.py:379
  360.8 5.2 %tri_sums.3 = bf16[8,16,32,128]{3,2,1,0:T(8,128)(2,1)} custom-call(bf16[8,16,32,512]{3,2,1,0:T(8,128)(2,1)} %all-to-all-done.l_ref, bf16[8,16,16,512]{3,2,1,0:T(8,128)(2,1)} %collective-permute-done.refs_0_), custom_call_target="tpu_custom_call" | custom-call | tf_op jit(solution)/shard_map/tri_sums/pallas_call | solution.py:203
  365.9 7.0 %all-to-all-start.2 = ((bf16[8,16,32,128]{3,2,1,0:T(8,128)(2,1)}), bf16[8,16,32,128]{3,2,1,0:T(8,128)(2,1)S(1)}, u32[]{:S(2)}, u32[]{:S(2)}) async-start(bf16[8,16,32,128]{3,2,1,0:T(8,128)(2,1)} %tri_sums.3), calls=%async_computation.2 | async-start | bytes 2097152 | tf_op jit(solution)/shard_map/all_to_all | solution.py:407
  373.0 1.4 slice.12.wg_ref
  377.5 1.3 copy.53
  378.8 14.8 %pair_tail.2.refs_0_ = f32[32,16,2,16,128]{4,3,2,1,0:T(8,128)} custom-call(s32[1]{0:T(128)} %bitcast.6.half_ref, bf16[32,16,2,16,128]{4,3,2,1,0:T(8,128)(2,1)} %bitcast.44, bf16[128,32,256]{2,1,0:T(8,128)(2,1)} %bitcast.29.tri_ref, bf16[128,128]{1,0:T(8,128)(2,1)} %slice.12.wg_ref, bf16[128,128]{1,0:T(8,128)(2,1)} %wt_ref.5, bf16[128,512]{1,0:T(8,128)(2,1)} %w1_ref.5, ...), custom_call_target="tpu_custom_call" | custom-call | tf_op jit(solution)/shard_map/pair_tail/pallas_call | solution.py:318
  393.6 8.5 %pair_tail.3 = f32[32,16,2,16,128]{4,3,2,1,0:T(8,128)} custom-call(s32[1]{0:T(128)S(6)} %sub.9.half_ref, bf16[32,16,2,16,128]{4,3,2,1,0:T(8,128)(2,1)} %bitcast.45, bf16[128,32,128]{2,1,0:T(8,128)(2,1)} %bitcast.52, bf16[128,128]{1,0:T(8,128)(2,1)} %slice.12.wg_ref, bf16[128,128]{1,0:T(8,128)(2,1)} %wt_ref.5, ...), custom_call_target="tpu_custom_call", output_to_operand_aliasing={{}: (7, {})} | custom-call | tf_op jit(solution)/shard_map/pair_tail/pallas_call | solution.py:318
  402.1 35.8 %opm_block.1 = (f32[32,512,128]{2,1,0:T(8,128)}, bf16[32,512,128]{2,1,0:T(8,128)(2,1)}) custom-call(bf16[32,128,32]{2,1,0:T(8,128)(2,1)} %bitcast.54, bf16[16,32,8,512]{3,2,1,0:T(8,128)(2,1)} %all-gather.15.cloned.1.call-done.r_ref, bf16[32,4096]{1,0:T(8,128)(2,1)} %reshape.89.w_ref, bf16[512,128]{1,0:T(8,128)(2,1)} %bitcast.66, f32[4,128,8]{2,1,0:T(8,128)} %bitcast.62, ...), custom_call_target="tpu_custom_call" | custom-call | tf_op jit(solution)/shard_map/opm_block/pallas_call | solution.py:251
  438.9 8.7 %pair_tail_last.1 = bf16[32,16,2,16,128]{4,3,2,1,0:T(8,128)(2,1)} custom-call(s32[1]{0:T(128)S(6)} %sub.9.half_ref, bf16[32,16,2,16,128]{4,3,2,1,0:T(8,128)(2,1)} %bitcast.46, bf16[128,32,128]{2,1,0:T(8,128)(2,1)} %bitcast.53, bf16[128,128]{1,0:T(8,128)(2,1)} %slice.12.wg_ref, bf16[128,128]{1,0:T(8,128)(2,1)} %wt_ref.5, ...), custom_call_target="tpu_custom_call", output_to_operand_aliasing={{}: (8, {})} | custom-call | tf_op jit(solution)/shard_map/pair_tail_last/pallas_call | solution.py:318
  (56 shorter events, 10.7 us)
Async XLA Ops:
  7.9 2.5 copy-start.11
  19.1 28.2 %all-to-all-start.1 = ((bf16[8,16,16,512]{3,2,1,0:T(8,128)(2,1)}), bf16[8,16,16,512]{3,2,1,0:T(8,128)(2,1)S(1)}, u32[]{:S(2)}, u32[]{:S(2)}) async-start(bf16[8,16,16,512]{3,2,1,0:T(8,128)(2,1)} %bitcast.58), calls=%async_computation.1 | async-start | bytes 4194304 | tf_op jit(solution)/shard_map/all_to_all | solution.py:369
  23.6 30.0 %copy-start.9 = (bf16[8,16,512]{2,1,0:T(8,128)(2,1)S(1)}, bf16[8,16,512]{2,1,0:T(8,128)(2,1)}, u32[]{:S(2)}) copy-start(bf16[8,16,512]{2,1,0:T(8,128)(2,1)} %get-tuple-element.12) | copy-start | bytes 393220
  32.5 21.1 %copy-start.10 = (bf16[8,16,512]{2,1,0:T(8,128)(2,1)S(1)}, bf16[8,16,512]{2,1,0:T(8,128)(2,1)}, u32[]{:S(2)}) copy-start(bf16[8,16,512]{2,1,0:T(8,128)(2,1)} %get-tuple-element.11) | copy-start | bytes 393220
  47.3 21.4 %copy-start = (bf16[8,16,16,512]{3,2,1,0:T(8,128)(2,1)}, bf16[8,16,16,512]{3,2,1,0:T(8,128)(2,1)S(1)}, u32[]{:S(2)}) copy-start(bf16[8,16,16,512]{3,2,1,0:T(8,128)(2,1)S(1)} %all-to-all-done.1.refs_1_) | copy-start | bytes 6291460
  47.3 44.9 %all-to-all-start.4 = ((bf16[8,16,16,512]{3,2,1,0:T(8,128)(2,1)}), bf16[8,16,16,512]{3,2,1,0:T(8,128)(2,1)}, u32[]{:S(2)}, u32[]{:S(2)}) async-start(bf16[8,16,16,512]{3,2,1,0:T(8,128)(2,1)} %bitcast.57), calls=%async_computation.4 | async-start | bytes 4194304 | tf_op jit(solution)/shard_map/all_to_all | solution.py:369
  53.6 47.3 %all-gather.9.cloned.1.call-start = ((), (), s32[]{:S(2)}) async-start(), calls=%async_computation.7 | async-start | bytes 1310720 | tf_op jit(solution)/shard_map/all_gather | solution.py:389
  92.2 10.1 %copy-start.7 = (s32[128,512]{1,0:T(8,128)S(1)}, s32[128,512]{1,0:T(8,128)}, u32[]{:S(2)}) copy-start(s32[128,512]{1,0:T(8,128)} %param.15) | copy-start | bytes 786436
  92.2 10.1 %copy-start.12 = (f32[512]{0:T(512)S(1)}, f32[512]{0:T(512)}, u32[]{:S(2)}) copy-start(f32[512]{0:T(512)} %copy-done.11) | copy-start | bytes 6148
  92.2 133.3 %all-to-all-start = ((bf16[8,16,32,512]{3,2,1,0:T(8,128)(2,1)}), bf16[8,16,32,512]{3,2,1,0:T(8,128)(2,1)}, u32[]{:S(2)}, u32[]{:S(2)}) async-start(bf16[8,16,32,512]{3,2,1,0:T(8,128)(2,1)} %bitcast.48), calls=%async_computation | async-start | bytes 8388608 | tf_op jit(solution)/shard_map/all_to_all | solution.py:369
  100.9 70.9 %all-gather.11.cloned.1.call-start = ((), (), s32[]{:S(2)}) async-start(), calls=%async_computation.8 | async-start | bytes 5242880 | tf_op jit(solution)/shard_map/all_gather | solution.py:390
  101.6 151.0 %all-gather.13.cloned.1.call-start = ((), (), s32[]{:S(2)}) async-start(), calls=%async_computation.9 | async-start | bytes 1310720 | tf_op jit(solution)/shard_map/all_gather | solution.py:389
  101.6 127.9 %collective-permute-start.1 = (bf16[8,16,16,512]{3,2,1,0:T(8,128)(2,1)}, bf16[8,16,16,512]{3,2,1,0:T(8,128)(2,1)S(1)}, u32[]{:S(2)}, u32[]{:S(2)}) collective-permute-start(bf16[8,16,16,512]{3,2,1,0:T(8,128)(2,1)} %all-to-all-done.4.refs_0_), channel_id=1, source_target_pairs={{0,8},{1,9},{2,10},{3,11},{4,12},{5,13},{6,14},{7,15},{8,0},{9,1},... | collective-permute-start | bytes 6291464 | tf_op jit(solution)/shard_map/ppermute | solution.py:379
  225.5 19.7 %all-to-all-start.3 = ((bf16[16,2,4096]{2,1,0:T(2,128)(2,1)}), bf16[16,2,4096]{2,1,0:T(2,128)(2,1)S(1)}, u32[]{:S(2)}, u32[]{:S(2)}) async-start(bf16[16,2,4096]{2,1,0:T(2,128)(2,1)} %reshape.106), calls=%async_computation.3 | async-start | bytes 524288 | tf_op jit(solution)/shard_map/all_to_all | solution.py:418
  229.6 1.3 copy-start.4
  245.2 0.7 copy-start.5
  245.9 18.0 %all-to-all-start.5 = ((bf16[8,16,32,128]{3,2,1,0:T(8,128)(2,1)}), bf16[8,16,32,128]{3,2,1,0:T(8,128)(2,1)S(1)}, u32[]{:S(2)}, u32[]{:S(2)}) async-start(bf16[8,16,32,128]{3,2,1,0:T(8,128)(2,1)} %tri_sums.4), calls=%async_computation.5 | async-start | bytes 2097152 | tf_op jit(solution)/shard_map/all_to_all | solution.py:407
  249.8 152.3 %all-gather.15.cloned.1.call-start = ((), (), s32[]{:S(2)}) async-start(), calls=%async_computation.10 | async-start | bytes 5242880 | tf_op jit(solution)/shard_map/all_gather | solution.py:390
  261.9 8.4 %copy-start.1 = (bf16[8,16,16,512]{3,2,1,0:T(8,128)(2,1)S(1)}, bf16[8,16,16,512]{3,2,1,0:T(8,128)(2,1)}, u32[]{:S(2)}) copy-start(bf16[8,16,16,512]{3,2,1,0:T(8,128)(2,1)} %copy-done) | copy-start | bytes 6291460
  263.8 102.1 %copy-start.2 = (bf16[8,16,32,128]{3,2,1,0:T(8,128)(2,1)}, bf16[8,16,32,128]{3,2,1,0:T(8,128)(2,1)S(1)}, u32[]{:S(2)}) copy-start(bf16[8,16,32,128]{3,2,1,0:T(8,128)(2,1)S(1)} %all-to-all-done.5) | copy-start | bytes 3145732
  263.9 102.1 %all-to-all-start.6 = ((bf16[8,16,32,256]{3,2,1,0:T(8,128)(2,1)}), bf16[8,16,32,256]{3,2,1,0:T(8,128)(2,1)}, u32[]{:S(2)}, u32[]{:S(2)}) async-start(bf16[8,16,32,256]{3,2,1,0:T(8,128)(2,1)} %tri_sums.5), calls=%async_computation.6 | async-start | bytes 4194304 | tf_op jit(solution)/shard_map/all_to_all | solution.py:407
  270.3 90.5 %collective-permute-start = (bf16[8,16,16,512]{3,2,1,0:T(8,128)(2,1)S(1)}, bf16[8,16,16,512]{3,2,1,0:T(8,128)(2,1)}, u32[]{:S(2)}, u32[]{:S(2)}) collective-permute-start(bf16[8,16,16,512]{3,2,1,0:T(8,128)(2,1)S(1)} %copy-done.1), channel_id=1, source_target_pairs={{0,8},{1,9},{2,10},{3,11},{4,12},{5,13},{6,14},{7,15},{8,0},{9,1},... | collective-permute-start | bytes 6291464 | tf_op jit(solution)/shard_map/ppermute | solution.py:379
  360.8 15.4 %copy-start.8 = (bf16[1024,128]{1,0:T(8,128)(2,1)S(1)}, bf16[1024,128]{1,0:T(8,128)(2,1)}, u32[]{:S(2)}) copy-start(bf16[1024,128]{1,0:T(8,128)(2,1)} %param.21) | copy-start | bytes 786436
  360.8 16.2 %copy-start.6 = (bf16[16,2,4096]{2,1,0:T(2,128)(2,1)S(1)}, bf16[16,2,4096]{2,1,0:T(2,128)(2,1)}, u32[]{:S(2)}) copy-start(bf16[16,2,4096]{2,1,0:T(2,128)(2,1)} %copy-done.5) | copy-start | bytes 786436
  365.9 71.9 %all-to-all-start.2 = ((bf16[8,16,32,128]{3,2,1,0:T(8,128)(2,1)}), bf16[8,16,32,128]{3,2,1,0:T(8,128)(2,1)S(1)}, u32[]{:S(2)}, u32[]{:S(2)}) async-start(bf16[8,16,32,128]{3,2,1,0:T(8,128)(2,1)} %tri_sums.3), calls=%async_computation.2 | async-start | bytes 2097152 | tf_op jit(solution)/shard_map/all_to_all | solution.py:407
  437.9 1.0 copy-start.3
Sparse Core Ops, SparseCore 0:
  56.5 39.6 all-gather.8
  103.2 68.4 all-gather.10
  222.2 30.4 all-gather.12
  255.6 57.9 all-gather.14

commit v3 on v2

--- a/solution.py
+++ b/solution.py
@@ -373,23 +373,34 @@
         for part in range(parts)
     ]
     bias = jnp.concatenate([b for _, b in made], axis=1)
+
+    planes = 4 if ring % 4 == 0 else 1
+    members = ring // planes
+    plane = place // members
+    within = [[m + members * z for m in range(members)] for z in range(planes)]
+    order = [m * planes + z for z in range(planes) for m in range(members)]
+
+    def across(values):
+        got = [values]
+        for k in range(1, planes):
+            got.append(lax.ppermute(values, "row", [(r, r ^ (k * members)) for r in range(ring)]))
+        got = jnp.stack(got)
+        return jnp.stack([lax.dynamic_index_in_dim(got, plane ^ z, 0, keepdims=False) for z in range(planes)])
+
+    def gather(values):
+        values = lax.all_gather(values, "row", axis=0, axis_index_groups=within)
+        return values.reshape((ring,) + values.shape[2:])
+
+    bias = across(bias)
     right_own, right_oth = [], []
     for part in range(parts):
-        right_own.append(spread(made[part][0]))
+        right = made[part][0]
+        if part:
+            right, bias = lax.optimization_barrier((right, bias))
+        right_own.append(spread(right))
         right_oth.append(lax.ppermute(right_own[part], "row", swap))
     (left,) = pair_head(coupling_features, my_residue, residue, trio[0 : 2 * cz])
     left_own = spread(left)
-    planes = 4 if ring % 4 == 0 else 1
-    members = ring // planes
-    across = [[m + members * z for z in range(planes)] for m in range(members)]
-    within = [[m + members * z for m in range(members)] for z in range(planes)]
-    order = [m * planes + z for z in range(planes) for m in range(members)]
-
-    def gather(values):
-        values = lax.all_gather(values, "row", axis=0, axis_index_groups=across)
-        values = lax.all_gather(values, "row", axis=0, axis_index_groups=within)
-        return values.reshape((ring,) + values.shape[2:])
-
     bias_all = gather(bias)
 
     msa_out, left_opm, right_opm = msa_block(
@@ -414,7 +425,7 @@
         sums = tri_sums(left_own, [right_oth[part]])
         tri_oth.append(collect(sums))
 
-    right_all = gather(right_opm.transpose(1, 0, 2))
+    right_all = gather(across(right_opm.transpose(1, 0, 2)))
     left_res = lax.all_to_all(left_opm, "row", split_axis=2, concat_axis=0, tiled=True).transpose(2, 0, 1)
     left_res = left_res.reshape(owned, planes, members, seqs, outer).transpose(0, 2, 1, 3, 4)
     left_res = left_res.reshape(owned, ring * seqs, outer)
@@ -439,6 +450,8 @@
 
 
 def solution(mesh):
+
+
     return jax.shard_map(
         functools.partial(body, mesh.shape["row"]),
         mesh=mesh,

time: 456 us -> 481 us (1.055)
  starting transfers between devices: 42.5 us -> 56.7 us
  waiting for transfers between devices: 211 us -> 218 us
    ppermute x0 -> x6, waiting for transfers between devices: none -> 48.2 us  [across(): lax.ppermute(values, 'row', [(r, r ^ k * members) for r in range(ring)])]
    all_to_all x3, waiting for transfers between devices: 38.3 us -> 9.49 us  [spread(): lax.all_to_all(values, 'row', 0, 0, tiled=True, axis_index_groups=halves)]
    all_to_all x3, starting transfers between devices: 17.3 us -> 24.5 us  [collect(): lax.all_to_all(sums, 'row', 0, 0, tiled=True, axis_index_groups=halves)]
    all_to_all x1, waiting for transfers between devices: 9.14 us -> 2.77 us  [body(): lax.all_to_all(left_opm, 'row', split_axis=2, concat_axis=0, tiled=True)]
    ppermute x0 -> x6, starting transfers between devices: none -> 6.27 us  [across(): lax.ppermute(values, 'row', [(r, r ^ k * members) for r in range(ring)])]
  transfers between devices with their start and end apart: 13 -> 17, of which waited for: 7 -> 9; matrix products, arithmetic and copies ran while one was open for 3% -> 4% of each run, Pallas kernels for 33% -> 31%
where the time goes in v3:
time: 481 us; the launch traced here: 479 us
  waiting for transfers between devices  218 us (45%)
  Pallas kernels  167 us (35%)
  starting transfers between devices  56.7 us (12%)
  local copies, waits for them, and re-layouts  21.4 us (4%)
  between operations  14.2 us (3%)
    ppermute x2, waiting for transfers between devices, body(): right_oth.append(lax.ppermute(right_own[part], 'row', swap))  89.9 us
    all_gather x2, waiting for transfers between devices, gather(): values = lax.all_gather(values, 'row', axis=0, axis_index_groups=within)  67 us
    pallas_call x1, Pallas kernels, msa_block(): pl.pallas_call(functools.partial(msa_kernel, width, divisor(res, 256), or...  50.2 us
    ppermute x6, waiting for transfers between devices, across(): lax.ppermute(values, 'row', [(r, r ^ k * members) for r in range(ring)])  48.2 us
    pallas_call x1, Pallas kernels, opm_block(): pl.pallas_call(opm_kernel, grid=(owned // rows,), in_specs=[pl.BlockSpec(...  35.8 us
    pallas_call x3, Pallas kernels, pair_tail(): pl.pallas_call(functools.partial(tail_kernel, last), grid_spec=pltpu.Pref...  32.1 us
    pallas_call x3, Pallas kernels, pair_head(): pl.pallas_call(kernel, grid=(steps,), in_specs=in_specs, out_specs=out_sp...  31.9 us
    all_to_all x3, starting transfers between devices, collect(): lax.all_to_all(sums, 'row', 0, 0, tiled=True, axis_index_groups=halves)  24.5 us
  transfers between devices with their start and end apart: 17, of which 9 were waited for; matrix products, arithmetic and copies ran while one was open for 4% of the time, Pallas kernels for 31%

profile of v3, /device:TPU:13, one launch (start us, length us, event | category | flops | bytes accessed | tf_op | source)
XLA Modules:
  0.0 479.2 jit_solution(11244701761212128942)
XLA Ops:
  10.3 8.8 %pair_head_bias.3 = (bf16[128,16,512]{2,1,0:T(8,128)(2,1)}, bf16[8,16,512]{2,1,0:T(8,128)(2,1)}) custom-call(bf16[32,512,128]{2,1,0:T(8,128)(2,1)} %x_ref.7, f32[2,1,16]{2,1,0:T(1,128)} %bitcast.89, f32[1,512]{1,0:T(1,128)} %bitcast.85, bf16[256,128]{1,0:T(8,128)(2,1)} %get-tuple-element.33.w_ref, bf16[8,128]{1,0:T(8,128)(2,1)} %bitcast.92), custom_call_target="tpu_custom_call" | custom-call | tf_op jit(solution)/shard_map/pair_head_bias/pallas_call | solution.py:100
  19.1 4.6 all-to-all-start.4
  23.7 8.8 %pair_head_bias.2 = (bf16[128,16,512]{2,1,0:T(8,128)(2,1)}, bf16[8,16,512]{2,1,0:T(8,128)(2,1)}) custom-call(bf16[32,512,128]{2,1,0:T(8,128)(2,1)} %x_ref.7, f32[2,1,16]{2,1,0:T(1,128)} %bitcast.90, f32[1,512]{1,0:T(1,128)} %bitcast.86, bf16[256,128]{1,0:T(8,128)(2,1)} %get-tuple-element.33.w_ref, bf16[8,128]{1,0:T(8,128)(2,1)} %bitcast.93), custom_call_target="tpu_custom_call" | custom-call | tf_op jit(solution)/shard_map/pair_head_bias/pallas_call | solution.py:100
  37.0 4.0 collective-permute-done.2
  41.0 19.7 %collective-permute-done.1 = bf16[8,32,512]{2,1,0:T(8,128)(2,1)S(1)} collective-permute-done((bf16[8,32,512]{2,1,0:T(8,128)(2,1)S(1)}, bf16[8,32,512]{2,1,0:T(8,128)(2,1)S(1)}, u32[]{:S(2)}, u32[]{:S(2)}) %collective-permute-start.1) | collective-permute-done | bytes 262176 | tf_op jit(solution)/shard_map/ppermute | solution.py:386
  60.7 3.6 collective-permute-done
  65.7 6.3 %all-to-all-start.1 = ((bf16[8,16,16,512]{3,2,1,0:T(8,128)(2,1)}), bf16[8,16,16,512]{3,2,1,0:T(8,128)(2,1)}, u32[]{:S(2)}, u32[]{:S(2)}) async-start(bf16[8,16,16,512]{3,2,1,0:T(8,128)(2,1)} %bitcast.65), calls=%async_computation.1 | async-start | bytes 4194304 | tf_op jit(solution)/shard_map/all_to_all | solution.py:369
  72.0 14.3 %pair_head.1 = bf16[128,32,512]{2,1,0:T(8,128)(2,1)} custom-call(bf16[32,512,128]{2,1,0:T(8,128)(2,1)} %x_ref.7, f32[2,1,16]{2,1,0:T(1,128)} %bitcast.91, f32[1,512]{1,0:T(1,128)} %bitcast.87, bf16[256,128]{1,0:T(8,128)(2,1)} %get-tuple-element.32.w_ref), custom_call_target="tpu_custom_call" | custom-call | tf_op jit(solution)/shard_map/pair_head/pallas_call | solution.py:100
  86.3 9.5 %all-to-all-done.1.refs_1_ = bf16[8,16,16,512]{3,2,1,0:T(8,128)(2,1)} async-done(((bf16[8,16,16,512]{3,2,1,0:T(8,128)(2,1)}), bf16[8,16,16,512]{3,2,1,0:T(8,128)(2,1)}, u32[]{:S(2)}, u32[]{:S(2)}) %all-to-all-start.1) | async-done | bytes 2097184 | tf_op jit(solution)/shard_map/all_to_all | solution.py:369
  95.8 6.6 %all-to-all-start = ((bf16[8,16,32,512]{3,2,1,0:T(8,128)(2,1)}), bf16[8,16,32,512]{3,2,1,0:T(8,128)(2,1)}, u32[]{:S(2)}, u32[]{:S(2)}) async-start(bf16[8,16,32,512]{3,2,1,0:T(8,128)(2,1)} %bitcast.55), calls=%async_computation | async-start | bytes 8388608 | tf_op jit(solution)/shard_map/all_to_all | solution.py:369
  103.1 2.4 collective-permute-start.7
  106.3 67.0 %all-gather.5.cloned.1.call-done.bias_ref = bf16[16,8,32,512]{3,2,1,0:T(8,128)(2,1)} async-done(((bf16[4,8,32,512]{3,2,1,0:T(8,128)(2,1)}), bf16[16,8,32,512]{3,2,1,0:T(8,128)(2,1)}) %all-gather.5.cloned.1.call-update) | async-done | bytes 4194320 | tf_op jit(solution)/shard_map/all_gather | solution.py:391
  173.3 50.2 %msa_block.1 = (bf16[8,512,256]{2,1,0:T(8,128)(2,1)}, bf16[8,32,512]{2,1,0:T(8,128)(2,1)}, bf16[8,32,512]{2,1,0:T(8,128)(2,1)}) custom-call(bf16[8,512,256]{2,1,0:T(8,128)(2,1)} %x_ref.6, f32[8,1,512]{2,1,0:T(1,128)} %reshape.78.valid_ref, bf16[16,8,32,512]{3,2,1,0:T(8,128)(2,1)} %all-gather.5.cloned.1.call-done.bias_ref, bf16[256,1024]{1,0:T(8,128)(2,1)} %w_ref.1, ...), custom_call_target="tpu_custom_call" | custom-call | tf_op jit(solution)/shard_map/msa_block/pallas_call | solution.py:158
  223.5 1.7 copy.50
  226.9 5.2 %all-to-all-start.3 = ((bf16[16,2,4096]{2,1,0:T(2,128)(2,1)}), bf16[16,2,4096]{2,1,0:T(2,128)(2,1)S(1)}, u32[]{:S(2)}, u32[]{:S(2)}) async-start(bf16[16,2,4096]{2,1,0:T(2,128)(2,1)} %reshape.104), calls=%async_computation.3 | async-start | bytes 524288 | tf_op jit(solution)/shard_map/all_to_all | solution.py:429
  232.1 5.2 %tri_sums.4 = bf16[8,16,32,128]{3,2,1,0:T(8,128)(2,1)} custom-call(bf16[8,16,32,512]{3,2,1,0:T(8,128)(2,1)} %all-to-all-done.l_ref, bf16[8,16,16,512]{3,2,1,0:T(8,128)(2,1)} %collective-permute-done.7.refs_0_), custom_call_target="tpu_custom_call" | custom-call | tf_op jit(solution)/shard_map/tri_sums/pallas_call | solution.py:203
  237.3 2.8 all-to-all-done.3
  240.1 5.7 %all-to-all-start.5 = ((bf16[8,16,32,128]{3,2,1,0:T(8,128)(2,1)}), bf16[8,16,32,128]{3,2,1,0:T(8,128)(2,1)S(1)}, u32[]{:S(2)}, u32[]{:S(2)}) async-start(bf16[8,16,32,128]{3,2,1,0:T(8,128)(2,1)} %tri_sums.4), calls=%async_computation.5 | async-start | bytes 2097152 | tf_op jit(solution)/shard_map/all_to_all | solution.py:418
  248.5 15.9 %collective-permute-done.5 = bf16[32,8,512]{2,0,1:T(8,128)(2,1)S(1)} collective-permute-done((bf16[32,8,512]{2,0,1:T(8,128)(2,1)S(1)}, bf16[32,8,512]{2,0,1:T(8,128)(2,1)S(1)}, u32[]{:S(2)}, u32[]{:S(2)}) %collective-permute-start.5) | collective-permute-done | bytes 262176 | tf_op jit(solution)/shard_map/ppermute | solution.py:386
  264.3 5.1 %collective-permute-done.4 = bf16[32,8,512]{2,0,1:T(8,128)(2,1)S(1)} collective-permute-done((bf16[32,8,512]{2,0,1:T(8,128)(2,1)S(1)}, bf16[32,8,512]{2,0,1:T(8,128)(2,1)S(1)}, u32[]{:S(2)}, u32[]{:S(2)}) %collective-permute-start.4) | collective-permute-done | bytes 262176 | tf_op jit(solution)/shard_map/ppermute | solution.py:386
  271.4 6.4 %tri_sums.5 = bf16[8,16,32,256]{3,2,1,0:T(8,128)(2,1)} custom-call(bf16[8,16,32,512]{3,2,1,0:T(8,128)(2,1)} %all-to-all-done.l_ref, bf16[8,16,16,512]{3,2,1,0:T(8,128)(2,1)} %copy-done, bf16[8,16,16,512]{3,2,1,0:T(8,128)(2,1)} %all-to-all-done.1.refs_1_), custom_call_target="tpu_custom_call" | custom-call | tf_op jit(solution)/shard_map/tri_sums/pallas_call | solution.py:203
  277.8 11.7 %all-to-all-start.6 = ((bf16[8,16,32,256]{3,2,1,0:T(8,128)(2,1)}), bf16[8,16,32,256]{3,2,1,0:T(8,128)(2,1)S(1)}, u32[]{:S(2)}, u32[]{:S(2)}) async-start(bf16[8,16,32,256]{3,2,1,0:T(8,128)(2,1)} %tri_sums.5), calls=%async_computation.6 | async-start | bytes 4194304 | tf_op jit(solution)/shard_map/all_to_all | solution.py:418
  290.3 89.9 %collective-permute-done.3.refs_0_ = bf16[8,16,16,512]{3,2,1,0:T(8,128)(2,1)} collective-permute-done((bf16[8,16,16,512]{3,2,1,0:T(8,128)(2,1)}, bf16[8,16,16,512]{3,2,1,0:T(8,128)(2,1)}, u32[]{:S(2)}, u32[]{:S(2)}) %collective-permute-start.3) | collective-permute-done | bytes 2097184 | tf_op jit(solution)/shard_map/ppermute | solution.py:401
  380.2 5.1 %tri_sums.3 = bf16[8,16,32,128]{3,2,1,0:T(8,128)(2,1)} custom-call(bf16[8,16,32,512]{3,2,1,0:T(8,128)(2,1)} %all-to-all-done.l_ref, bf16[8,16,16,512]{3,2,1,0:T(8,128)(2,1)} %collective-permute-done.3.refs_0_), custom_call_target="tpu_custom_call" | custom-call | tf_op jit(solution)/shard_map/tri_sums/pallas_call | solution.py:203
  385.3 7.1 %all-to-all-start.2 = ((bf16[8,16,32,128]{3,2,1,0:T(8,128)(2,1)}), bf16[8,16,32,128]{3,2,1,0:T(8,128)(2,1)S(1)}, u32[]{:S(2)}, u32[]{:S(2)}) async-start(bf16[8,16,32,128]{3,2,1,0:T(8,128)(2,1)} %tri_sums.3), calls=%async_computation.2 | async-start | bytes 2097152 | tf_op jit(solution)/shard_map/all_to_all | solution.py:418
  396.5 1.8 reshape.89.w_ref
  398.3 2.7 reshape.105
  401.0 2.5 copy.53
  403.5 14.8 %pair_tail.2.refs_0_ = f32[32,16,2,16,128]{4,3,2,1,0:T(8,128)} custom-call(s32[1]{0:T(128)} %bitcast.9.half_ref, bf16[32,16,2,16,128]{4,3,2,1,0:T(8,128)(2,1)} %bitcast.51, bf16[128,32,256]{2,1,0:T(8,128)(2,1)} %bitcast.57, bf16[128,128]{1,0:T(8,128)(2,1)} %slice.12.wg_ref, bf16[128,128]{1,0:T(8,128)(2,1)} %wt_ref.5, bf16[128,512]{1,0:T(8,128)(2,1)} %w1_ref.5, ...), custom_call_target="tpu_custom_call" | custom-call | tf_op jit(solution)/shard_map/pair_tail/pallas_call | solution.py:318
  418.4 8.5 %pair_tail.3 = f32[32,16,2,16,128]{4,3,2,1,0:T(8,128)} custom-call(s32[1]{0:T(128)S(6)} %sub.13.half_ref, bf16[32,16,2,16,128]{4,3,2,1,0:T(8,128)(2,1)} %bitcast.52, bf16[128,32,128]{2,1,0:T(8,128)(2,1)} %bitcast.60, bf16[128,128]{1,0:T(8,128)(2,1)} %slice.12.wg_ref, bf16[128,128]{1,0:T(8,128)(2,1)} %wt_ref.5, ...), custom_call_target="tpu_custom_call", output_to_operand_aliasing={{}: (7, {})} | custom-call | tf_op jit(solution)/shard_map/pair_tail/pallas_call | solution.py:318
  426.9 35.8 %opm_block.1 = (f32[32,512,128]{2,1,0:T(8,128)}, bf16[32,512,128]{2,1,0:T(8,128)(2,1)}) custom-call(bf16[32,128,32]{2,1,0:T(8,128)(2,1)} %bitcast.62, bf16[16,32,8,512]{3,2,1,0:T(8,128)(2,1)} %all-gather.7.cloned.1.call-done.r_ref, bf16[32,4096]{1,0:T(8,128)(2,1)} %reshape.89.w_ref, bf16[512,128]{1,0:T(8,128)(2,1)} %bitcast.73, f32[4,128,8]{2,1,0:T(8,128)} %bitcast.70, ...), custom_call_target="tpu_custom_call" | custom-call | tf_op jit(solution)/shard_map/opm_block/pallas_call | solution.py:251
  463.6 8.7 %pair_tail_last.1 = bf16[32,16,2,16,128]{4,3,2,1,0:T(8,128)(2,1)} custom-call(s32[1]{0:T(128)S(6)} %sub.13.half_ref, bf16[32,16,2,16,128]{4,3,2,1,0:T(8,128)(2,1)} %bitcast.53, bf16[128,32,128]{2,1,0:T(8,128)(2,1)} %bitcast.61, bf16[128,128]{1,0:T(8,128)(2,1)} %slice.12.wg_ref, bf16[128,128]{1,0:T(8,128)(2,1)} %wt_ref.5, ...), custom_call_target="tpu_custom_call", output_to_operand_aliasing={{}: (8, {})} | custom-call | tf_op jit(solution)/shard_map/pair_tail_last/pallas_call | solution.py:318
  (65 shorter events, 22.7 us)
Async XLA Ops:
  7.9 2.5 copy-start.9
  19.1 13.4 %copy-start.8 = (bf16[8,16,512]{2,1,0:T(8,128)(2,1)S(1)}, bf16[8,16,512]{2,1,0:T(8,128)(2,1)}, u32[]{:S(2)}) copy-start(bf16[8,16,512]{2,1,0:T(8,128)(2,1)} %get-tuple-element.14) | copy-start | bytes 393220
  19.1 46.5 %all-to-all-start.4 = ((bf16[8,16,16,512]{3,2,1,0:T(8,128)(2,1)}), bf16[8,16,16,512]{3,2,1,0:T(8,128)(2,1)S(1)}, u32[]{:S(2)}, u32[]{:S(2)}) async-start(bf16[8,16,16,512]{3,2,1,0:T(8,128)(2,1)} %bitcast.66), calls=%async_computation.4 | async-start | bytes 4194304 | tf_op jit(solution)/shard_map/all_to_all | solution.py:369
  33.5 7.5 %collective-permute-start.2 = (bf16[8,32,512]{2,1,0:T(8,128)(2,1)S(1)}, bf16[8,32,512]{2,1,0:T(8,128)(2,1)S(1)}, u32[]{:S(2)}, u32[]{:S(2)}) collective-permute-start(bf16[8,32,512]{2,1,0:T(8,128)(2,1)S(1)} %constant_dynamic-update-slice_fusion), channel_id=1, source_target_pairs={{0,12},{1,13},{2,14},{3,15},{4,8},{5,9},{6,10},{7,11},{8,4},{9,5},... | collective-permute-start | bytes 786440 | tf_op jit(solution)/shard_map/ppermute | solution.py:386
  35.0 25.7 %collective-permute-start.1 = (bf16[8,32,512]{2,1,0:T(8,128)(2,1)S(1)}, bf16[8,32,512]{2,1,0:T(8,128)(2,1)S(1)}, u32[]{:S(2)}, u32[]{:S(2)}) collective-permute-start(bf16[8,32,512]{2,1,0:T(8,128)(2,1)S(1)} %constant_dynamic-update-slice_fusion), channel_id=1, source_target_pairs={{0,8},{1,9},{2,10},{3,11},{4,12},{5,13},{6,14},{7,15},{8,0},{9,1},... | collective-permute-start | bytes 786440 | tf_op jit(solution)/shard_map/ppermute | solution.py:386
  35.9 28.3 %collective-permute-start = (bf16[8,32,512]{2,1,0:T(8,128)(2,1)S(1)}, bf16[8,32,512]{2,1,0:T(8,128)(2,1)S(1)}, u32[]{:S(2)}, u32[]{:S(2)}) collective-permute-start(bf16[8,32,512]{2,1,0:T(8,128)(2,1)S(1)} %constant_dynamic-update-slice_fusion), channel_id=1, source_target_pairs={{0,4},{1,5},{2,6},{3,7},{4,0},{5,1},{6,2},{7,3},{8,12},{9,13},{10,... | collective-permute-start | bytes 786440 | tf_op jit(solution)/shard_map/ppermute | solution.py:386
  65.7 37.5 %copy-start = (bf16[8,16,16,512]{3,2,1,0:T(8,128)(2,1)}, bf16[8,16,16,512]{3,2,1,0:T(8,128)(2,1)S(1)}, u32[]{:S(2)}) copy-start(bf16[8,16,16,512]{3,2,1,0:T(8,128)(2,1)S(1)} %all-to-all-done.4.refs_0_) | copy-start | bytes 6291460
  65.7 30.1 %all-to-all-start.1 = ((bf16[8,16,16,512]{3,2,1,0:T(8,128)(2,1)}), bf16[8,16,16,512]{3,2,1,0:T(8,128)(2,1)}, u32[]{:S(2)}, u32[]{:S(2)}) async-start(bf16[8,16,16,512]{3,2,1,0:T(8,128)(2,1)} %bitcast.65), calls=%async_computation.1 | async-start | bytes 4194304 | tf_op jit(solution)/shard_map/all_to_all | solution.py:369
  95.7 9.8 %copy-start.6 = (s32[128,512]{1,0:T(8,128)S(1)}, s32[128,512]{1,0:T(8,128)}, u32[]{:S(2)}) copy-start(s32[128,512]{1,0:T(8,128)} %param.15) | copy-start | bytes 786436
  95.7 9.8 %copy-start.10 = (f32[512]{0:T(512)S(1)}, f32[512]{0:T(512)}, u32[]{:S(2)}) copy-start(f32[512]{0:T(512)} %copy-done.9) | copy-start | bytes 6148
  95.8 131.2 %all-to-all-start = ((bf16[8,16,32,512]{3,2,1,0:T(8,128)(2,1)}), bf16[8,16,32,512]{3,2,1,0:T(8,128)(2,1)}, u32[]{:S(2)}, u32[]{:S(2)}) async-start(bf16[8,16,32,512]{3,2,1,0:T(8,128)(2,1)} %bitcast.55), calls=%async_computation | async-start | bytes 8388608 | tf_op jit(solution)/shard_map/all_to_all | solution.py:369
  102.4 70.9 %all-gather.5.cloned.1.call-start = ((), (), s32[]{:S(2)}) async-start(), calls=%async_computation.7 | async-start | bytes 5242880 | tf_op jit(solution)/shard_map/all_gather | solution.py:391
  103.1 129.0 %collective-permute-start.7 = (bf16[8,16,16,512]{3,2,1,0:T(8,128)(2,1)S(1)}, bf16[8,16,16,512]{3,2,1,0:T(8,128)(2,1)}, u32[]{:S(2)}, u32[]{:S(2)}) collective-permute-start(bf16[8,16,16,512]{3,2,1,0:T(8,128)(2,1)S(1)} %all-to-all-done.4.refs_0_), channel_id=1, source_target_pairs={{0,8},{1,9},{2,10},{3,11},{4,12},{5,13},{6,14},{7,15},{8,0},{9,1},... | collective-permute-start | bytes 6291464 | tf_op jit(solution)/shard_map/ppermute | solution.py:401
  105.5 121.4 %copy-start.4 = (f32[128,512]{1,0:T(8,128)}, f32[128,512]{1,0:T(8,128)S(1)}, u32[]{:S(2)}) copy-start(f32[128,512]{1,0:T(8,128)S(1)} %convert_multiply_fusion) | copy-start | bytes 786436
  226.9 13.2 %all-to-all-start.3 = ((bf16[16,2,4096]{2,1,0:T(2,128)(2,1)}), bf16[16,2,4096]{2,1,0:T(2,128)(2,1)S(1)}, u32[]{:S(2)}, u32[]{:S(2)}) async-start(bf16[16,2,4096]{2,1,0:T(2,128)(2,1)} %reshape.104), calls=%async_computation.3 | async-start | bytes 524288 | tf_op jit(solution)/shard_map/all_to_all | solution.py:429
  232.1 13.6 %copy-start.7 = (bf16[8,32,512]{2,1,0:T(8,128)(2,1)S(1)}, bf16[8,32,512]{2,1,0:T(8,128)(2,1)}, u32[]{:S(2)}) copy-start(bf16[8,32,512]{2,1,0:T(8,128)(2,1)} %get-tuple-element.20) | copy-start | bytes 786436
  240.1 29.8 %copy-start.5 = (bf16[16,2,4096]{2,1,0:T(2,128)(2,1)}, bf16[16,2,4096]{2,1,0:T(2,128)(2,1)S(1)}, u32[]{:S(2)}) copy-start(bf16[16,2,4096]{2,1,0:T(2,128)(2,1)S(1)} %all-to-all-done.3) | copy-start | bytes 786436
  240.1 37.8 %all-to-all-start.5 = ((bf16[8,16,32,128]{3,2,1,0:T(8,128)(2,1)}), bf16[8,16,32,128]{3,2,1,0:T(8,128)(2,1)S(1)}, u32[]{:S(2)}, u32[]{:S(2)}) async-start(bf16[8,16,32,128]{3,2,1,0:T(8,128)(2,1)} %tri_sums.4), calls=%async_computation.5 | async-start | bytes 2097152 | tf_op jit(solution)/shard_map/all_to_all | solution.py:418
  245.7 181.1 %all-gather.7.cloned.1.call-start = ((), (), s32[]{:S(2)}) async-start(), calls=%async_computation.8 | async-start | bytes 5242880 | tf_op jit(solution)/shard_map/all_gather | solution.py:391
  245.7 18.6 %collective-permute-start.5 = (bf16[32,8,512]{2,0,1:T(8,128)(2,1)S(1)}, bf16[32,8,512]{2,0,1:T(8,128)(2,1)S(1)}, u32[]{:S(2)}, u32[]{:S(2)}) collective-permute-start(bf16[32,8,512]{2,0,1:T(8,128)(2,1)S(1)} %bitcast.77), channel_id=1, source_target_pairs={{0,8},{1,9},{2,10},{3,11},{4,12},{5,13},{6,14},{7,15},{8,0},{9,1},... | collective-permute-start | bytes 786440 | tf_op jit(solution)/shard_map/ppermute | solution.py:386
  246.6 22.8 %collective-permute-start.4 = (bf16[32,8,512]{2,0,1:T(8,128)(2,1)S(1)}, bf16[32,8,512]{2,0,1:T(8,128)(2,1)S(1)}, u32[]{:S(2)}, u32[]{:S(2)}) collective-permute-start(bf16[32,8,512]{2,0,1:T(8,128)(2,1)S(1)} %bitcast.78), channel_id=1, source_target_pairs={{0,4},{1,5},{2,6},{3,7},{4,0},{5,1},{6,2},{7,3},{8,12},{9,13},{10,... | collective-permute-start | bytes 786440 | tf_op jit(solution)/shard_map/ppermute | solution.py:386
  246.8 22.6 %collective-permute-start.6 = (bf16[32,8,512]{2,0,1:T(8,128)(2,1)S(1)}, bf16[32,8,512]{2,0,1:T(8,128)(2,1)S(1)}, u32[]{:S(2)}, u32[]{:S(2)}) collective-permute-start(bf16[32,8,512]{2,0,1:T(8,128)(2,1)S(1)} %bitcast.79), channel_id=1, source_target_pairs={{0,12},{1,13},{2,14},{3,15},{4,8},{5,9},{6,10},{7,11},{8,4},{9,5},... | collective-permute-start | bytes 786440 | tf_op jit(solution)/shard_map/ppermute | solution.py:386
  277.8 107.5 %copy-start.2 = (bf16[8,16,32,128]{3,2,1,0:T(8,128)(2,1)}, bf16[8,16,32,128]{3,2,1,0:T(8,128)(2,1)S(1)}, u32[]{:S(2)}) copy-start(bf16[8,16,32,128]{3,2,1,0:T(8,128)(2,1)S(1)} %all-to-all-done.5) | copy-start | bytes 3145732
  277.8 107.5 %all-to-all-start.6 = ((bf16[8,16,32,256]{3,2,1,0:T(8,128)(2,1)}), bf16[8,16,32,256]{3,2,1,0:T(8,128)(2,1)S(1)}, u32[]{:S(2)}, u32[]{:S(2)}) async-start(bf16[8,16,32,256]{3,2,1,0:T(8,128)(2,1)} %tri_sums.5), calls=%async_computation.6 | async-start | bytes 4194304 | tf_op jit(solution)/shard_map/all_to_all | solution.py:418
  289.6 90.6 %collective-permute-start.3 = (bf16[8,16,16,512]{3,2,1,0:T(8,128)(2,1)}, bf16[8,16,16,512]{3,2,1,0:T(8,128)(2,1)}, u32[]{:S(2)}, u32[]{:S(2)}) collective-permute-start(bf16[8,16,16,512]{3,2,1,0:T(8,128)(2,1)} %all-to-all-done.1.refs_1_), channel_id=1, source_target_pairs={{0,8},{1,9},{2,10},{3,11},{4,12},{5,13},{6,14},{7,15},{8,0},{9,1},... | collective-permute-start | bytes 6291464 | tf_op jit(solution)/shard_map/ppermute | solution.py:401
  385.3 18.2 %copy-start.1 = (bf16[8,16,32,256]{3,2,1,0:T(8,128)(2,1)}, bf16[8,16,32,256]{3,2,1,0:T(8,128)(2,1)S(1)}, u32[]{:S(2)}) copy-start(bf16[8,16,32,256]{3,2,1,0:T(8,128)(2,1)S(1)} %all-to-all-done.6) | copy-start | bytes 6291460
  385.3 77.3 %all-to-all-start.2 = ((bf16[8,16,32,128]{3,2,1,0:T(8,128)(2,1)}), bf16[8,16,32,128]{3,2,1,0:T(8,128)(2,1)S(1)}, u32[]{:S(2)}, u32[]{:S(2)}) async-start(bf16[8,16,32,128]{3,2,1,0:T(8,128)(2,1)} %tri_sums.3), calls=%async_computation.2 | async-start | bytes 2097152 | tf_op jit(solution)/shard_map/all_to_all | solution.py:418
  462.6 1.0 copy-start.3
Sparse Core Ops, SparseCore 0:
  104.7 68.4 all-gather.4
  271.6 63.1 all-gather.6

commit v4 on v3

--- a/solution.py
+++ b/solution.py
@@ -210,7 +210,7 @@
     )(left, *rights)
 
 
-def opm_kernel(l_ref, r_ref, w_ref, vt_ref, vi_ref, two_ref, o_ref, sum_ref, mix, right):
+def opm_kernel(l_ref, r_ref, w_ref, vt_ref, vi_ref, o_ref, mix, right):
     rows, seqs, outer = l_ref.shape
     owners, inner, local, res = r_ref.shape
     cz = o_ref.shape[2]
@@ -237,12 +237,10 @@
         for n in range(pair):
             mine = jnp.broadcast_to(vi_ref[:, first + n : first + n + 1], (seqs, cz)).astype(BF16)
             tally = jnp.maximum(dot(vt_ref[...], mine), 1.0)
-            mean = total[:, n * cz : (n + 1) * cz] / tally
-            o_ref[first + n] = mean
-            sum_ref[first + n] = (mean + two_ref[first + n]).astype(BF16)
-
-
-def opm_block(left, right, w, valid_t, mine, two):
+            o_ref[first + n] = total[:, n * cz : (n + 1) * cz] / tally
+
+
+def opm_block(left, right, w, valid_t, mine):
     owned, seqs, outer = left.shape
     _, inner, _, res = right.shape
     cz = w.shape[1] // inner
@@ -257,20 +255,15 @@
             full(w.shape),
             full(valid_t.shape),
             pl.BlockSpec((None, seqs, rows), lambda g: (g, 0, 0)),
-            pair,
         ],
-        out_specs=[pair, pair],
-        out_shape=[
-            jax.ShapeDtypeStruct((owned, res, cz), F32),
-            jax.ShapeDtypeStruct((owned, res, cz), BF16),
-        ],
+        out_specs=pair,
+        out_shape=jax.ShapeDtypeStruct((owned, res, cz), F32),
         scratch_shapes=[pltpu.VMEM((seqs * inner, 2 * cz), BF16), pltpu.VMEM((res, seqs * inner), BF16)],
         name="opm_block",
-    )(left, right, w, valid_t, mine.reshape(seqs, owned // rows, rows).transpose(1, 0, 2), two)
-
-
-def tail_kernel(last, half_ref, x_ref, tri_ref, wg_ref, wt_ref, w1_ref, w2_ref, *refs):
-    opm_ref = refs[0]
+    )(left, right, w, valid_t, mine.reshape(seqs, owned // rows, rows).transpose(1, 0, 2))
+
+
+def tail_kernel(table_ref, x_ref, tri_ref, opm_ref, wg_ref, wt_ref, w1_ref, w2_ref, *refs):
     o_ref, scr = refs[-2:]
     rows, groups, lines, cz = x_ref.shape
     cols = groups * lines
@@ -286,47 +279,41 @@
         tri = [dot(norm(get_rows(scr, i + m, rows), 0).astype(BF16), wt_ref[...], 0, 0) for m in range(many)]
         one = x + gate * jnp.concatenate(tri, axis=0)
         hidden = jnp.maximum(dot(norm(one).astype(BF16), w1_ref[...]), 0.0).astype(BF16)
-        out = one + dot(hidden, w2_ref[...])
-        if last:
-            out = out + opm_ref[pl.ds(i, many)].reshape(many * cols, cz)
+        out = one + dot(hidden, w2_ref[...]) + opm_ref[pl.ds(i, many)].reshape(many * cols, cz)
         o_ref[pl.ds(i, many)] = out.astype(o_ref.dtype).reshape(many, groups, lines, cz)
         return carry
 
     lax.fori_loop(0, rows // many, block, 0, unroll=TAIL_UNROLL)
 
 
-def pair_tail(half, first, parts, x, tri, weights, opm=None, earlier=None):
+def pair_tail(table, parts, x, tri, opm, weights, earlier=None):
     owned, res, cz = x.shape
     ring = res // owned
     rows = divisor(owned, 16)
     lines = owned // parts
     span = ring // 2 * lines
-    count = tri.shape[2] // span
-    last = opm is not None
     view = (owned, ring, parts, lines, cz)
-    pair = pl.BlockSpec((rows, ring // 2, None, lines, cz), lambda q, g, h: (g, h[0], first + q, 0, 0))
-    in_specs = [pair, pl.BlockSpec((cz, rows, span), lambda q, g, h: (0, g, q))] + [full(w.shape) for w in weights]
-    args = [half, x.reshape(view), tri, *weights]
-    if last:
-        in_specs.append(pair)
-        args.append(opm.reshape(view))
+    pair = pl.BlockSpec((rows, ring // 2, None, lines, cz), lambda q, g, t: (g, t[0, q], t[1, q], 0, 0))
+    in_specs = [pair, pl.BlockSpec((cz, rows, span), lambda q, g, t: (0, g, q)), pair]
+    in_specs += [full(w.shape) for w in weights]
+    args = [table, x.reshape(view), tri, opm.reshape(view), *weights]
     aliases = {}
     if earlier is not None:
         aliases = {len(args): 0}
         in_specs.append(pl.BlockSpec(memory_space=pl.ANY))
         args.append(earlier.reshape(view))
     return pl.pallas_call(
-        functools.partial(tail_kernel, last),
+        tail_kernel,
         grid_spec=pltpu.PrefetchScalarGridSpec(
             num_scalar_prefetch=1,
-            grid=(count, owned // rows),
+            grid=(tri.shape[2] // span, owned // rows),
             in_specs=in_specs,
             out_specs=pair,
             scratch_shapes=[pltpu.VMEM((max(span // LANES, 1), cz * rows, min(span, LANES)), F32)],
         ),
-        out_shape=jax.ShapeDtypeStruct(view, BF16 if last else F32),
+        out_shape=jax.ShapeDtypeStruct(view, BF16),
         input_output_aliases=aliases,
-        name="pair_tail_last" if last else "pair_tail",
+        name="pair_tail",
     )(*args).reshape(owned, res, cz)
 
 
@@ -362,7 +349,7 @@
     trio = trio_factor_matrices.T
 
     parts = 2 if owned % 32 == 0 else 1
-    half = (place // near).astype(jnp.int32).reshape(1)
+    half = (place // near).astype(jnp.int32)
 
     def spread(values):
         values = values.reshape(near, cz // near, values.shape[1], values.shape[-1])
@@ -381,9 +368,9 @@
     order = [m * planes + z for z in range(planes) for m in range(members)]
 
     def across(values):
-        got = [values]
+        got = [values[0]]
         for k in range(1, planes):
-            got.append(lax.ppermute(values, "row", [(r, r ^ (k * members)) for r in range(ring)]))
+            got.append(lax.ppermute(values[k], "row", [(r, r ^ (k * members)) for r in range(ring)]))
         got = jnp.stack(got)
         return jnp.stack([lax.dynamic_index_in_dim(got, plane ^ z, 0, keepdims=False) for z in range(planes)])
 
@@ -391,7 +378,7 @@
         values = lax.all_gather(values, "row", axis=0, axis_index_groups=within)
         return values.reshape((ring,) + values.shape[2:])
 
-    bias = across(bias)
+    bias = across([bias] * planes)
     right_own, right_oth = [], []
     for part in range(parts):
         right = made[part][0]
@@ -418,34 +405,34 @@
         back = lax.all_to_all(sums, "row", 0, 0, tiled=True, axis_index_groups=halves)
         return back.reshape(cz, owned, sums.shape[-1])
 
-    sums = tri_sums(left_own, right_own)
-    tri_own = collect(sums)
-    tri_oth = []
-    for part in range(parts):
-        sums = tri_sums(left_own, [right_oth[part]])
-        tri_oth.append(collect(sums))
-
-    right_all = gather(across(right_opm.transpose(1, 0, 2)))
-    left_res = lax.all_to_all(left_opm, "row", split_axis=2, concat_axis=0, tiled=True).transpose(2, 0, 1)
-    left_res = left_res.reshape(owned, planes, members, seqs, outer).transpose(0, 2, 1, 3, 4)
-    left_res = left_res.reshape(owned, ring * seqs, outer)
+    spot = res // planes
+    both = []
+    for k in range(planes):
+        lines = lax.dynamic_slice_in_dim(left_opm, (plane ^ k) * spot, spot, 2)
+        both.append(jnp.concatenate([right_opm, lines], axis=2).transpose(1, 0, 2))
+    both = gather(across(both))
+    right_all = both[..., 0:res]
+    left_res = lax.dynamic_slice_in_dim(both, res + (place % members) * owned, owned, 3)
+    left_res = left_res.transpose(3, 0, 2, 1).reshape(owned, ring * seqs, outer)
     entry_order = entry.reshape(planes, members, seqs, res).transpose(1, 0, 2, 3).reshape(ring * seqs, res)
     mine = lax.dynamic_slice_in_dim(entry_order, place * owned, owned, 1)
-    weights = (trio_factor_matrices[:, 4 * cz : 5 * cz], trio_final_matrix, feedforward_expand, feedforward_shrink)
-    two = pair_tail(half, 0, parts, coupling_features, tri_own, weights)
-    for part in range(parts - 1):
-        two = pair_tail(1 - half, part, parts, coupling_features, tri_oth[part], weights, earlier=two)
-    opm, pair = opm_block(
+    opm = opm_block(
         left_res,
         right_all,
         product_final_matrix.reshape(outer, outer * cz),
         entry_order.T.astype(BF16),
         mine,
-        two,
     )
-    pair = pair_tail(
-        1 - half, parts - 1, parts, coupling_features, tri_oth[-1], weights, opm=opm, earlier=pair
-    )
+
+    sums = tri_sums(left_own, right_own + right_oth[:-1])
+    tri_near = collect(sums)
+    sums = tri_sums(left_own, right_oth[-1:])
+    tri_last = collect(sums)
+    weights = (trio_factor_matrices[:, 4 * cz : 5 * cz], trio_final_matrix, feedforward_expand, feedforward_shrink)
+    table = jnp.array([[0] * parts + [1] * parts, list(range(parts)) * 2], jnp.int32)
+    table = table.at[0].set(table[0] ^ half)
+    pair = pair_tail(table[:, :-1], parts, coupling_features, tri_near, opm, weights)
+    pair = pair_tail(table[:, -1:], parts, coupling_features, tri_last, opm, weights, earlier=pair)
     return (msa_out, pair)
 
 

time: 481 us -> 447 us (0.929)
  waiting for transfers between devices: 218 us -> 197 us
  starting transfers between devices: 56.7 us -> 43.8 us
  Pallas kernels: 167 us -> 162 us
    all_gather x2, waiting for transfers between devices: 67 us -> 38.1 us  [gather(): values = lax.all_gather(values, 'row', axis=0, axis_index_groups=within)]
    all_to_all x3 -> x2, starting transfers between devices: 24.5 us -> 13.4 us  [collect(): lax.all_to_all(sums, 'row', 0, 0, tiled=True, axis_index_groups=halves)]
    all_to_all x3, starting transfers between devices: 17.6 us -> 24.1 us  [spread(): lax.all_to_all(values, 'row', 0, 0, tiled=True, axis_index_groups=halves)]
    all_to_all x3, waiting for transfers between devices: 9.49 us -> 15.5 us  [spread(): lax.all_to_all(values, 'row', 0, 0, tiled=True, axis_index_groups=halves)]
    unnamed x26 -> x23, local copies, waits for them, and re-layouts: 6.5 us -> 1.12 us
    all_to_all x1 -> x0, starting transfers between devices: 5.22 us -> none  [body(): lax.all_to_all(left_opm, 'row', split_axis=2, concat_axis=0, tiled=True)]
    slice x0 -> x2, local copies, waits for them, and re-layouts: none -> 5.22 us  [the longest x1 4.57 us: body(): right_all = both[..., 0:res]]
    pallas_call x3 -> x2, Pallas kernels: 16.7 us -> 12.8 us  [tri_sums(): pl.pallas_call(tri_kernel, grid=(chans // step,), in_specs=[spec(owned, r...]
  transfers between devices with their start and end apart: 17 -> 15, of which waited for: 9 -> 8; matrix products, arithmetic and copies ran while one was open for 4% -> 6% of each run, Pallas kernels for 31% -> 32%
where the time goes in v4:
time: 447 us; the launch traced here: 445 us
  waiting for transfers between devices  197 us (44%)
  Pallas kernels  162 us (36%)
  starting transfers between devices  43.8 us (10%)
  local copies, waits for them, and re-layouts  24.4 us (5%)
  between operations  14.3 us (3%)
    ppermute x2, waiting for transfers between devices, body(): right_oth.append(lax.ppermute(right_own[part], 'row', swap))  89.9 us
    ppermute x6, waiting for transfers between devices, across(): lax.ppermute(values[k], 'row', [(r, r ^ k * members) for r in range(ring)])  52.7 us
    pallas_call x1, Pallas kernels, msa_block(): pl.pallas_call(functools.partial(msa_kernel, width, divisor(res, 256), or...  50.2 us
    all_gather x2, waiting for transfers between devices, gather(): values = lax.all_gather(values, 'row', axis=0, axis_index_groups=within)  38.1 us
    pallas_call x1, Pallas kernels, opm_block(): pl.pallas_call(opm_kernel, grid=(owned // rows,), in_specs=[pl.BlockSpec(...  34.8 us
    pallas_call x2, Pallas kernels, pair_tail(): pl.pallas_call(tail_kernel, grid_spec=pltpu.PrefetchScalarGridSpec(num_sc...  32 us
    pallas_call x3, Pallas kernels, pair_head(): pl.pallas_call(kernel, grid=(steps,), in_specs=in_specs, out_specs=out_sp...  32 us
    all_to_all x3, starting transfers between devices, spread(): lax.all_to_all(values, 'row', 0, 0, tiled=True, axis_index_groups=halves)  24.1 us
  transfers between devices with their start and end apart: 15, of which 8 were waited for; matrix products, arithmetic and copies ran while one was open for 6% of the time, Pallas kernels for 32%

profile of v4, /device:TPU:13, one launch (start us, length us, event | category | flops | bytes accessed | tf_op | source)
XLA Modules:
  0.0 444.6 jit_solution(7858326336525798422)
XLA Ops:
  8.5 1.1 copy.63
  10.3 8.8 %pair_head_bias.3 = (bf16[128,16,512]{2,1,0:T(8,128)(2,1)}, bf16[8,16,512]{2,1,0:T(8,128)(2,1)}) custom-call(bf16[32,512,128]{2,1,0:T(8,128)(2,1)} %x_ref.7, f32[2,1,16]{2,1,0:T(1,128)} %bitcast.72, f32[1,512]{1,0:T(1,128)} %bitcast.67, bf16[256,128]{1,0:T(8,128)(2,1)} %get-tuple-element.49.w_ref, bf16[8,128]{1,0:T(8,128)(2,1)} %bitcast.75), custom_call_target="tpu_custom_call" | custom-call | tf_op jit(solution)/shard_map/pair_head_bias/pallas_call | solution.py:100
  19.1 4.5 %all-to-all-start.3 = ((bf16[8,16,16,512]{3,2,1,0:T(8,128)(2,1)}), bf16[8,16,16,512]{3,2,1,0:T(8,128)(2,1)S(1)}, u32[]{:S(2)}, u32[]{:S(2)}) async-start(bf16[8,16,16,512]{3,2,1,0:T(8,128)(2,1)} %bitcast.52), calls=%async_computation.3 | async-start | bytes 4194304 | tf_op jit(solution)/shard_map/all_to_all | solution.py:356
  23.6 8.9 %pair_head_bias.2 = (bf16[128,16,512]{2,1,0:T(8,128)(2,1)}, bf16[8,16,512]{2,1,0:T(8,128)(2,1)}) custom-call(bf16[32,512,128]{2,1,0:T(8,128)(2,1)} %x_ref.7, f32[2,1,16]{2,1,0:T(1,128)} %bitcast.73, f32[1,512]{1,0:T(1,128)} %bitcast.68, bf16[256,128]{1,0:T(8,128)(2,1)} %get-tuple-element.49.w_ref, bf16[8,128]{1,0:T(8,128)(2,1)} %bitcast.76), custom_call_target="tpu_custom_call" | custom-call | tf_op jit(solution)/shard_map/pair_head_bias/pallas_call | solution.py:100
  33.8 2.3 collective-permute-start.1
  36.1 21.3 %collective-permute-done = bf16[8,32,512]{2,1,0:T(8,128)(2,1)S(1)} collective-permute-done((bf16[8,32,512]{2,1,0:T(8,128)(2,1)S(1)}, bf16[8,32,512]{2,1,0:T(8,128)(2,1)S(1)}, u32[]{:S(2)}, u32[]{:S(2)}) %collective-permute-start) | collective-permute-done | bytes 262176 | tf_op jit(solution)/shard_map/ppermute | solution.py:373
  57.5 3.0 collective-permute-done.1
  60.8 1.1 pad_maximum_fusion.3
  61.9 11.9 %all-to-all-start.1 = ((bf16[8,16,16,512]{3,2,1,0:T(8,128)(2,1)}), bf16[8,16,16,512]{3,2,1,0:T(8,128)(2,1)}, u32[]{:S(2)}, u32[]{:S(2)}) async-start(bf16[8,16,16,512]{3,2,1,0:T(8,128)(2,1)} %bitcast.51), calls=%async_computation.1 | async-start | bytes 4194304 | tf_op jit(solution)/shard_map/all_to_all | solution.py:356
  74.5 14.3 %pair_head.1 = bf16[128,32,512]{2,1,0:T(8,128)(2,1)} custom-call(bf16[32,512,128]{2,1,0:T(8,128)(2,1)} %x_ref.7, f32[2,1,16]{2,1,0:T(1,128)} %bitcast.74, f32[1,512]{1,0:T(1,128)} %bitcast.69, bf16[256,128]{1,0:T(8,128)(2,1)} %get-tuple-element.48.w_ref), custom_call_target="tpu_custom_call" | custom-call | tf_op jit(solution)/shard_map/pair_head/pallas_call | solution.py:100
  88.8 15.5 %all-to-all-done.1.refs_1_ = bf16[8,16,16,512]{3,2,1,0:T(8,128)(2,1)} async-done(((bf16[8,16,16,512]{3,2,1,0:T(8,128)(2,1)}), bf16[8,16,16,512]{3,2,1,0:T(8,128)(2,1)}, u32[]{:S(2)}, u32[]{:S(2)}) %all-to-all-start.1) | async-done | bytes 2097184 | tf_op jit(solution)/shard_map/all_to_all | solution.py:356
  104.3 7.8 %all-to-all-start = ((bf16[8,16,32,512]{3,2,1,0:T(8,128)(2,1)}), bf16[8,16,32,512]{3,2,1,0:T(8,128)(2,1)}, u32[]{:S(2)}, u32[]{:S(2)}) async-start(bf16[8,16,32,512]{3,2,1,0:T(8,128)(2,1)} %bitcast.47), calls=%async_computation | async-start | bytes 8388608 | tf_op jit(solution)/shard_map/all_to_all | solution.py:356
  113.0 38.1 %all-gather.5.cloned.1.call-done.bias_ref = bf16[16,8,32,512]{3,2,1,0:T(8,128)(2,1)} async-done(((bf16[4,8,32,512]{3,2,1,0:T(8,128)(2,1)}), bf16[16,8,32,512]{3,2,1,0:T(8,128)(2,1)}) %all-gather.5.cloned.1.call-update) | async-done | bytes 4194320 | tf_op jit(solution)/shard_map/all_gather | solution.py:378
  151.0 50.2 %msa_block.1 = (bf16[8,512,256]{2,1,0:T(8,128)(2,1)}, bf16[8,32,512]{2,1,0:T(8,128)(2,1)}, bf16[8,32,512]{2,1,0:T(8,128)(2,1)}) custom-call(bf16[8,512,256]{2,1,0:T(8,128)(2,1)} %x_ref.6, f32[8,1,512]{2,1,0:T(1,128)} %reshape.88.valid_ref, bf16[16,8,32,512]{3,2,1,0:T(8,128)(2,1)} %all-gather.5.cloned.1.call-done.bias_ref, bf16[256,1024]{1,0:T(8,128)(2,1)} %w_ref.1, ...), custom_call_target="tpu_custom_call" | custom-call | tf_op jit(solution)/shard_map/msa_block/pallas_call | solution.py:158
  203.5 2.6 collective-permute-start.6
  206.0 7.8 %collective-permute-done.4 = bf16[32,8,640]{2,0,1:T(8,128)(2,1)S(1)} collective-permute-done((bf16[32,8,640]{2,0,1:T(8,128)(2,1)S(1)}, bf16[32,8,640]{2,0,1:T(8,128)(2,1)S(1)}, u32[]{:S(2)}, u32[]{:S(2)}) %collective-permute-start.4) | collective-permute-done | bytes 327712 | tf_op jit(solution)/shard_map/ppermute | solution.py:373
  213.9 3.2 collective-permute-done.5
  217.1 17.3 %collective-permute-done.6 = bf16[32,8,640]{2,0,1:T(8,128)(2,1)S(1)} collective-permute-done((bf16[32,8,640]{2,0,1:T(8,128)(2,1)S(1)}, bf16[32,8,640]{2,0,1:T(8,128)(2,1)S(1)}, u32[]{:S(2)}, u32[]{:S(2)}) %collective-permute-start.6) | collective-permute-done | bytes 327712 | tf_op jit(solution)/shard_map/ppermute | solution.py:373
  234.9 1.5 copy.67
  236.5 7.7 %tri_sums.3 = bf16[8,16,32,384]{3,2,1,0:T(8,128)(2,1)} custom-call(bf16[8,16,32,512]{3,2,1,0:T(8,128)(2,1)} %all-to-all-done.l_ref, bf16[8,16,16,512]{3,2,1,0:T(8,128)(2,1)} %copy-done.1, bf16[8,16,16,512]{3,2,1,0:T(8,128)(2,1)} %all-to-all-done.1.refs_1_, bf16[8,16,16,512]{3,2,1,0:T(8,128)(2,1)} %collective-permute-done.7.refs_2_), custom_call_target="tpu_custom_call" | custom-call | tf_op jit(solution)/shard_map/tri_sums/pallas_call | solution.py:203
  244.2 5.6 %all-to-all-start.4 = ((bf16[8,16,32,384]{3,2,1,0:T(8,128)(2,1)}), bf16[8,16,32,384]{3,2,1,0:T(8,128)(2,1)S(1)}, u32[]{:S(2)}, u32[]{:S(2)}) async-start(bf16[8,16,32,384]{3,2,1,0:T(8,128)(2,1)} %tri_sums.3), calls=%async_computation.4 | async-start | bytes 6291456 | tf_op jit(solution)/shard_map/all_to_all | solution.py:405
  250.7 89.9 %collective-permute-done.3.refs_0_ = bf16[8,16,16,512]{3,2,1,0:T(8,128)(2,1)} collective-permute-done((bf16[8,16,16,512]{3,2,1,0:T(8,128)(2,1)}, bf16[8,16,16,512]{3,2,1,0:T(8,128)(2,1)}, u32[]{:S(2)}, u32[]{:S(2)}) %collective-permute-start.3) | collective-permute-done | bytes 2097184 | tf_op jit(solution)/shard_map/ppermute | solution.py:388
  340.6 5.1 %tri_sums.2 = bf16[8,16,32,128]{3,2,1,0:T(8,128)(2,1)} custom-call(bf16[8,16,32,512]{3,2,1,0:T(8,128)(2,1)} %all-to-all-done.l_ref, bf16[8,16,16,512]{3,2,1,0:T(8,128)(2,1)} %collective-permute-done.3.refs_0_), custom_call_target="tpu_custom_call" | custom-call | tf_op jit(solution)/shard_map/tri_sums/pallas_call | solution.py:203
  345.7 7.7 %all-to-all-start.2 = ((bf16[8,16,32,128]{3,2,1,0:T(8,128)(2,1)}), bf16[8,16,32,128]{3,2,1,0:T(8,128)(2,1)}, u32[]{:S(2)}, u32[]{:S(2)}) async-start(bf16[8,16,32,128]{3,2,1,0:T(8,128)(2,1)} %tri_sums.2), calls=%async_computation.2 | async-start | bytes 2097152 | tf_op jit(solution)/shard_map/all_to_all | solution.py:405
  353.4 1.4 slice.42.wg_ref
  357.5 1.8 reshape.97.w_ref
  360.1 2.6 dynamic-slice_bitcast_fusion
  362.7 3.7 copy.68
  366.4 4.6 %slice.46.r_ref = bf16[16,32,8,512]{3,2,1,0:T(8,128)(2,1)} slice(bf16[16,32,8,640]{3,2,1,0:T(8,128)(2,1)} %all-gather.7.cloned.1.call-done), slice={[0:16], [0:32], [0:8], [0:512]} | slice | bytes 8388608 | tf_op jit(solution)/shard_map/slice | solution.py:414
  371.0 34.8 %opm_block.1 = f32[32,512,128]{2,1,0:T(8,128)} custom-call(bf16[32,128,32]{2,1,0:T(8,128)(2,1)} %bitcast.50, bf16[16,32,8,512]{3,2,1,0:T(8,128)(2,1)} %slice.46.r_ref, bf16[32,4096]{1,0:T(8,128)(2,1)} %reshape.97.w_ref, bf16[512,128]{1,0:T(8,128)(2,1)} %bitcast.59, f32[4,128,8]{2,1,0:T(8,128)} %bitcast.56), custom_call_target="tpu_custom_call" | custom-call | tf_op jit(solution)/shard_map/opm_block/pallas_call | solution.py:249
  405.8 22.4 %pair_tail.2.refs_0_ = bf16[32,16,2,16,128]{4,3,2,1,0:T(8,128)(2,1)} custom-call(s32[2,3]{1,0:T(2,128)} %bitcast.71, bf16[32,16,2,16,128]{4,3,2,1,0:T(8,128)(2,1)} %bitcast.43, bf16[128,32,384]{2,1,0:T(8,128)(2,1)} %bitcast.49, f32[32,16,2,16,128]{4,3,2,1,0:T(8,128)} %bitcast.45, bf16[128,128]{1,0:T(8,128)(2,1)} %slice.42.wg_ref, bf16[128,128]{1,0:T(8,128)(2,1)} %wt_ref.3, ...), custom_call_target="tpu_custom_call" | custom-call | tf_op jit(solution)/shard_map/pair_tail/pallas_call | solution.py:305
  428.1 9.7 %pair_tail.3 = bf16[32,16,2,16,128]{4,3,2,1,0:T(8,128)(2,1)} custom-call(s32[2,1]{1,0:T(2,128)} %slice.39.table_ref, bf16[32,16,2,16,128]{4,3,2,1,0:T(8,128)(2,1)} %bitcast.44, bf16[128,32,128]{2,1,0:T(8,128)(2,1)} %bitcast.12.tri_ref, f32[32,16,2,16,128]{4,3,2,1,0:T(8,128)} %bitcast.46, ...), custom_call_target="tpu_custom_call", output_to_operand_aliasing={{}: (8, {})} | custom-call | tf_op jit(solution)/shard_map/pair_tail/pallas_call | solution.py:305
  (62 shorter events, 12.3 us)
Async XLA Ops:
  7.9 2.4 copy-start.5
  19.1 42.8 %all-to-all-start.3 = ((bf16[8,16,16,512]{3,2,1,0:T(8,128)(2,1)}), bf16[8,16,16,512]{3,2,1,0:T(8,128)(2,1)S(1)}, u32[]{:S(2)}, u32[]{:S(2)}) async-start(bf16[8,16,16,512]{3,2,1,0:T(8,128)(2,1)} %bitcast.52), calls=%async_computation.3 | async-start | bytes 4194304 | tf_op jit(solution)/shard_map/all_to_all | solution.py:356
  23.6 8.9 %copy-start.4 = (bf16[8,16,512]{2,1,0:T(8,128)(2,1)S(1)}, bf16[8,16,512]{2,1,0:T(8,128)(2,1)}, u32[]{:S(2)}) copy-start(bf16[8,16,512]{2,1,0:T(8,128)(2,1)} %get-tuple-element.24) | copy-start | bytes 393220
  33.4 24.1 %collective-permute-start = (bf16[8,32,512]{2,1,0:T(8,128)(2,1)S(1)}, bf16[8,32,512]{2,1,0:T(8,128)(2,1)S(1)}, u32[]{:S(2)}, u32[]{:S(2)}) collective-permute-start(bf16[8,32,512]{2,1,0:T(8,128)(2,1)S(1)} %constant_dynamic-update-slice_fusion), channel_id=1, source_target_pairs={{0,4},{1,5},{2,6},{3,7},{4,0},{5,1},{6,2},{7,3},{8,12},{9,13},{10,... | collective-permute-start | bytes 786440 | tf_op jit(solution)/shard_map/ppermute | solution.py:373
  33.8 26.8 %collective-permute-start.1 = (bf16[8,32,512]{2,1,0:T(8,128)(2,1)S(1)}, bf16[8,32,512]{2,1,0:T(8,128)(2,1)S(1)}, u32[]{:S(2)}, u32[]{:S(2)}) collective-permute-start(bf16[8,32,512]{2,1,0:T(8,128)(2,1)S(1)} %constant_dynamic-update-slice_fusion), channel_id=1, source_target_pairs={{0,8},{1,9},{2,10},{3,11},{4,12},{5,13},{6,14},{7,15},{8,0},{9,1},... | collective-permute-start | bytes 786440 | tf_op jit(solution)/shard_map/ppermute | solution.py:373
  36.1 24.4 %collective-permute-start.2 = (bf16[8,32,512]{2,1,0:T(8,128)(2,1)S(1)}, bf16[8,32,512]{2,1,0:T(8,128)(2,1)S(1)}, u32[]{:S(2)}, u32[]{:S(2)}) collective-permute-start(bf16[8,32,512]{2,1,0:T(8,128)(2,1)S(1)} %constant_dynamic-update-slice_fusion), channel_id=1, source_target_pairs={{0,12},{1,13},{2,14},{3,15},{4,8},{5,9},{6,10},{7,11},{8,4},{9,5},... | collective-permute-start | bytes 786440 | tf_op jit(solution)/shard_map/ppermute | solution.py:373
  61.9 50.2 %copy-start.1 = (bf16[8,16,16,512]{3,2,1,0:T(8,128)(2,1)}, bf16[8,16,16,512]{3,2,1,0:T(8,128)(2,1)S(1)}, u32[]{:S(2)}) copy-start(bf16[8,16,16,512]{3,2,1,0:T(8,128)(2,1)S(1)} %all-to-all-done.3.refs_0_) | copy-start | bytes 6291460
  61.9 42.4 %all-to-all-start.1 = ((bf16[8,16,16,512]{3,2,1,0:T(8,128)(2,1)}), bf16[8,16,16,512]{3,2,1,0:T(8,128)(2,1)}, u32[]{:S(2)}, u32[]{:S(2)}) async-start(bf16[8,16,16,512]{3,2,1,0:T(8,128)(2,1)} %bitcast.51), calls=%async_computation.1 | async-start | bytes 4194304 | tf_op jit(solution)/shard_map/all_to_all | solution.py:356
  73.8 77.2 %all-gather.5.cloned.1.call-start = ((), (), s32[]{:S(2)}) async-start(), calls=%async_computation.5 | async-start | bytes 5242880 | tf_op jit(solution)/shard_map/all_gather | solution.py:378
  104.3 7.9 %copy-start.3 = (s32[128,512]{1,0:T(8,128)S(1)}, s32[128,512]{1,0:T(8,128)}, u32[]{:S(2)}) copy-start(s32[128,512]{1,0:T(8,128)} %param.18) | copy-start | bytes 786436
  104.3 7.9 %copy-start.6 = (f32[512]{0:T(512)S(1)}, f32[512]{0:T(512)}, u32[]{:S(2)}) copy-start(f32[512]{0:T(512)} %copy-done.5) | copy-start | bytes 6148
  104.3 132.1 %all-to-all-start = ((bf16[8,16,32,512]{3,2,1,0:T(8,128)(2,1)}), bf16[8,16,32,512]{3,2,1,0:T(8,128)(2,1)}, u32[]{:S(2)}, u32[]{:S(2)}) async-start(bf16[8,16,32,512]{3,2,1,0:T(8,128)(2,1)} %bitcast.47), calls=%async_computation | async-start | bytes 8388608 | tf_op jit(solution)/shard_map/all_to_all | solution.py:356
  112.1 248.0 %all-gather.7.cloned.1.call-start = ((), (), s32[]{:S(2)}) async-start(), calls=%async_computation.6 | async-start | bytes 6553600 | tf_op jit(solution)/shard_map/all_gather | solution.py:378
  112.1 124.3 %collective-permute-start.7 = (bf16[8,16,16,512]{3,2,1,0:T(8,128)(2,1)S(1)}, bf16[8,16,16,512]{3,2,1,0:T(8,128)(2,1)}, u32[]{:S(2)}, u32[]{:S(2)}) collective-permute-start(bf16[8,16,16,512]{3,2,1,0:T(8,128)(2,1)S(1)} %all-to-all-done.3.refs_0_), channel_id=1, source_target_pairs={{0,8},{1,9},{2,10},{3,11},{4,12},{5,13},{6,14},{7,15},{8,0},{9,1},... | collective-permute-start | bytes 6291464 | tf_op jit(solution)/shard_map/ppermute | solution.py:388
  112.3 89.0 %copy-start.2 = (f32[128,512]{1,0:T(8,128)}, f32[128,512]{1,0:T(8,128)S(1)}, u32[]{:S(2)}) copy-start(f32[128,512]{1,0:T(8,128)S(1)} %convert_multiply_fusion) | copy-start | bytes 786436
  203.3 10.6 %collective-permute-start.4 = (bf16[32,8,640]{2,0,1:T(8,128)(2,1)S(1)}, bf16[32,8,640]{2,0,1:T(8,128)(2,1)S(1)}, u32[]{:S(2)}, u32[]{:S(2)}) collective-permute-start(bf16[32,8,640]{2,0,1:T(8,128)(2,1)S(1)} %get-tuple-element.41), channel_id=1, source_target_pairs={{0,4},{1,5},{2,6},{3,7},{4,0},{5,1},{6,2},{7,3},{8,12},{9,13},{10,... | collective-permute-start | bytes 983048 | tf_op jit(solution)/shard_map/ppermute | solution.py:373
  203.4 13.7 %collective-permute-start.5 = (bf16[32,8,640]{2,0,1:T(8,128)(2,1)S(1)}, bf16[32,8,640]{2,0,1:T(8,128)(2,1)S(1)}, u32[]{:S(2)}, u32[]{:S(2)}) collective-permute-start(bf16[32,8,640]{2,0,1:T(8,128)(2,1)S(1)} %get-tuple-element.42), channel_id=1, source_target_pairs={{0,8},{1,9},{2,10},{3,11},{4,12},{5,13},{6,14},{7,15},{8,0},{9,1},... | collective-permute-start | bytes 983048 | tf_op jit(solution)/shard_map/ppermute | solution.py:373
  203.5 30.9 %collective-permute-start.6 = (bf16[32,8,640]{2,0,1:T(8,128)(2,1)S(1)}, bf16[32,8,640]{2,0,1:T(8,128)(2,1)S(1)}, u32[]{:S(2)}, u32[]{:S(2)}) collective-permute-start(bf16[32,8,640]{2,0,1:T(8,128)(2,1)S(1)} %get-tuple-element.43), channel_id=1, source_target_pairs={{0,12},{1,13},{2,14},{3,15},{4,8},{5,9},{6,10},{7,11},{8,4},{9,5},... | collective-permute-start | bytes 983048 | tf_op jit(solution)/shard_map/ppermute | solution.py:373
  244.2 101.4 %all-to-all-start.4 = ((bf16[8,16,32,384]{3,2,1,0:T(8,128)(2,1)}), bf16[8,16,32,384]{3,2,1,0:T(8,128)(2,1)S(1)}, u32[]{:S(2)}, u32[]{:S(2)}) async-start(bf16[8,16,32,384]{3,2,1,0:T(8,128)(2,1)} %tri_sums.3), calls=%async_computation.4 | async-start | bytes 6291456 | tf_op jit(solution)/shard_map/all_to_all | solution.py:405
  249.9 90.7 %collective-permute-start.3 = (bf16[8,16,16,512]{3,2,1,0:T(8,128)(2,1)}, bf16[8,16,16,512]{3,2,1,0:T(8,128)(2,1)}, u32[]{:S(2)}, u32[]{:S(2)}) collective-permute-start(bf16[8,16,16,512]{3,2,1,0:T(8,128)(2,1)} %all-to-all-done.1.refs_1_), channel_id=1, source_target_pairs={{0,8},{1,9},{2,10},{3,11},{4,12},{5,13},{6,14},{7,15},{8,0},{9,1},... | collective-permute-start | bytes 6291464 | tf_op jit(solution)/shard_map/ppermute | solution.py:388
  345.6 13.6 %copy-start.8 = (s32[2,4]{1,0:T(2,128)S(1)}, s32[2,4]{1,0:T(2,128)}, u32[]{:S(2)}) copy-start(s32[2,4]{1,0:T(2,128)} %constant.103.clone) | copy-start | bytes 100
  345.6 13.6 %copy-start.9 = (s32[1,4]{1,0:T(1,128)S(1)}, s32[1,4]{1,0:T(1,128)}, u32[]{:S(2)}) copy-start(s32[1,4]{1,0:T(1,128)} %constant.105) | copy-start | bytes 52
  345.6 17.1 %copy-start = (bf16[8,16,32,384]{3,2,1,0:T(8,128)(2,1)}, bf16[8,16,32,384]{3,2,1,0:T(8,128)(2,1)S(1)}, u32[]{:S(2)}) copy-start(bf16[8,16,32,384]{3,2,1,0:T(8,128)(2,1)S(1)} %all-to-all-done.4) | copy-start | bytes 9437188
  345.7 82.5 %all-to-all-start.2 = ((bf16[8,16,32,128]{3,2,1,0:T(8,128)(2,1)}), bf16[8,16,32,128]{3,2,1,0:T(8,128)(2,1)}, u32[]{:S(2)}, u32[]{:S(2)}) async-start(bf16[8,16,32,128]{3,2,1,0:T(8,128)(2,1)} %tri_sums.2), calls=%async_computation.2 | async-start | bytes 2097152 | tf_op jit(solution)/shard_map/all_to_all | solution.py:405
  359.5 7.0 %copy-start.7 = (s32[2,4]{1,0:T(2,128)}, s32[2,4]{1,0:T(2,128)S(1)}, u32[]{:S(2)}) copy-start(s32[2,4]{1,0:T(2,128)S(1)} %scatter.4) | copy-start | bytes 100
Sparse Core Ops, SparseCore 0:
  76.2 74.8 all-gather.4
  236.6 73.4 all-gather.6
